TPU v7x, 1024 devices: a whole 8x8x8 slice. The times are simulated.
1024 devices in a mesh: expert: 16 (over x, z_lo), block: 64 (over z_hi, y, core).
Axes of the slice: x: 8, y: 8, z: 8 (z_hi: 4, z_lo: 2; z = z_hi * 2 + z_lo), core: 2. Of those that a mesh axis runs over, the one named last changes fastest.
Arguments:
- iterate: bfloat16 [16, 7168, 2048], P(None, ('expert', 'block')), may hold values from -0.046875 to 0.046875
Outputs:
- update: bfloat16 [16, 64, 448, 512], P('expert', 'block')
All inputs are finite; a program needn't handle non-finite values.
Results may differ from a plain program's by a relative error of at most 0.015.
Values may be sent and summed in bfloat16 or wider, within the bound.
No kernel may reach another device: no remote copies, remote signals or barrier semaphores. Data moves between devices by JAX's collectives and lax.ppermute only.
A program may use at most 32 MiB of HBM per device.

v0:
```python
import math

import jax
import jax.numpy as jnp
from jax import lax
from jax.sharding import PartitionSpec as P

D = 7168
MOE_FF = 2048


def partner(value, axis, bit):
    mask = 2**bit
    pairs = [(source, source ^ mask) for source in range(lax.axis_size(axis))]
    return lax.ppermute(value, axis, pairs)


def gather_columns_group(piece, index, joined):
    for bit in (0, 1):
        other = partner(piece, "block", bit)
        upper = index >> bit & 1 == 1
        piece = jnp.where(
            upper, jnp.concatenate([other, piece], joined), jnp.concatenate([piece, other], joined)
        )
    return piece


def shards(iterate):
    index = lax.axis_index("block")
    levels = lax.axis_size("block").bit_length() - 1
    local = lax.all_to_all(iterate, "expert", split_axis=0, concat_axis=1, tiled=True)
    own_rows = local[0]
    row_block = gather_columns_group(own_rows, index, 0)
    width = row_block.shape[1] // 4
    column = index % 4
    mine = lax.dynamic_slice_in_dim(row_block, column * width, width, 1)
    grid_bits = list(range(2, levels))
    partial_value = lax.dot_general(
        mine, row_block, (((0,), (0,)), ((), ())), preferred_element_type=jnp.float32
    )
    partial_value = lax.optimization_barrier(partial_value.astype(jnp.bfloat16))
    summed = partial_value.astype(jnp.float32)
    for bit in grid_bits:
        half = summed.shape[1] // 2
        upper = index >> bit & 1 == 1
        lower_part = summed[:, :half]
        upper_part = summed[:, half:]
        keep = jnp.where(upper, upper_part, lower_part)
        outgoing = jnp.where(upper, lower_part, upper_part).astype(jnp.bfloat16)
        incoming = partner(outgoing, "block", bit)
        summed = keep + incoming.astype(jnp.float32)
    gram_rows = summed.astype(jnp.bfloat16)
    for bit in grid_bits[::-1]:
        incoming = partner(gram_rows, "block", bit)
        upper = index >> bit & 1 == 1
        gram_rows = jnp.where(
            upper,
            jnp.concatenate([incoming, gram_rows], 1),
            jnp.concatenate([gram_rows, incoming], 1),
        )
    first = lax.dot_general(
        row_block, gram_rows, (((1,), (1,)), ((), ())), preferred_element_type=jnp.float32
    )
    first = first.astype(jnp.bfloat16)
    first_rows = gather_columns_group(first, index, 1)
    second = lax.dot_general(
        first_rows, gram_rows, (((1,), (1,)), ((), ())), preferred_element_type=jnp.float32
    )
    scale = 0.2 * math.sqrt(max(D, MOE_FF))
    fresh = scale * (
        3.4445 * mine.astype(jnp.float32) - 4.775 * first.astype(jnp.float32) + 2.0315 * second
    )
    return fresh.astype(jnp.bfloat16)[None, None]


def solution(mesh):
    return jax.shard_map(
        shards,
        mesh=mesh,
        in_specs=(P(None, ("expert", "block"), None),),
        out_specs=P("expert", "block", None, None),
        check_vma=False,
    )
```

profile of v0, /device:TPU:1, one launch (start us, length us, event | category | flops | bytes accessed | tf_op | source)
XLA Modules:
  0.0 306.6 jit_solution(6635450192509259657)
XLA Ops:
  0.0 1.3 copy.4
  1.3 21.8 %all_to_all.4 = bf16[16,7,2048]{2,1,0:T(8,128)(2,1)S(1)} all-to-all(bf16[16,7,2048]{2,1,0:T(8,128)(2,1)S(1)} %copy.4), channel_id=1, replica_groups=mesh['expert'=16,'block'=64] {'expert'}, dimensions={0} | all-to-all | bytes 917504 | tf_op jit(solution)/shard_map/all_to_all | solution.py:31
  23.1 0.2 squeeze.3
  23.3 10.5 %collective-permute-start = (bf16[112,2048]{1,0:T(8,128)(2,1)S(1)}, bf16[112,2048]{1,0:T(8,128)(2,1)S(1)}, u32[]{:S(2)}, u32[]{:S(2)}) collective-permute-start(bf16[112,2048]{1,0:T(8,128)(2,1)S(1)} %squeeze.3), channel_id=1, source_target_pairs={{0,1},{1,0},{2,3},{3,2},{4,5},{5,4},{6,7},{7,6},{8,9},{9,8},{10,11... | collective-permute-start | bytes 1376264 | tf_op jit(solution)/shard_map/ppermute | solution.py:15
  33.8 1.4 collective-permute-done
  35.2 0.2 maximum_select_fusion.7
  35.4 1.9 collective-permute-start.1
  37.4 21.5 %collective-permute-done.1 = bf16[224,2048]{1,0:T(8,128)(2,1)S(1)} collective-permute-done((bf16[224,2048]{1,0:T(8,128)(2,1)S(1)}, bf16[224,2048]{1,0:T(8,128)(2,1)S(1)}, u32[]{:S(2)}, u32[]{:S(2)}) %collective-permute-start.1) | collective-permute-done | bytes 917536 | tf_op jit(solution)/shard_map/ppermute | solution.py:15
  58.9 0.7 maximum_select_fusion.1
  59.6 0.0 copy-start.1
  59.6 1.3 convolution_convert_fusion
  60.9 0.0 copy-done.1
  60.9 0.5 convert_element_type.47
  61.5 0.0 copy-start
  61.5 1.9 copy-done
  63.4 0.2 select_convert_fusion
  63.6 2.2 collective-permute-start.2
  65.8 48.1 %collective-permute-done.2 = bf16[512,1024]{1,0:T(8,128)(2,1)S(1)} collective-permute-done((bf16[512,1024]{1,0:T(8,128)(2,1)S(1)}, bf16[512,1024]{1,0:T(8,128)(2,1)S(1)}, u32[]{:S(2)}, u32[]{:S(2)}) %collective-permute-start.2) | collective-permute-done | bytes 1048608 | tf_op jit(solution)/shard_map/ppermute | solution.py:15
  113.9 2.8 convert_add_fusion
  116.7 0.1 select_convert_fusion.1
  116.9 5.4 %collective-permute-start.3 = (bf16[512,512]{1,0:T(8,128)(2,1)S(1)}, bf16[512,512]{1,0:T(8,128)(2,1)}, u32[]{:S(2)}, u32[]{:S(2)}) collective-permute-start(bf16[512,512]{1,0:T(8,128)(2,1)S(1)} %select_convert_fusion.1), channel_id=1, source_target_pairs={{0,8},{1,9},{2,10},{3,11},{4,12},{5,13},{6,14},{7,15},{8,0},{9,1},... | collective-permute-start | bytes 1572872 | tf_op jit(solution)/shard_map/ppermute | solution.py:15
  122.3 25.1 %collective-permute-done.3 = bf16[512,512]{1,0:T(8,128)(2,1)} collective-permute-done((bf16[512,512]{1,0:T(8,128)(2,1)S(1)}, bf16[512,512]{1,0:T(8,128)(2,1)}, u32[]{:S(2)}, u32[]{:S(2)}) %collective-permute-start.3) | collective-permute-done | bytes 524320 | tf_op jit(solution)/shard_map/ppermute | solution.py:15
  147.4 1.3 convert_add_fusion.1
  148.8 5.5 %collective-permute-start.4 = (bf16[512,256]{1,0:T(8,128)(2,1)S(1)}, bf16[512,256]{1,0:T(8,128)(2,1)S(1)}, u32[]{:S(2)}, u32[]{:S(2)}) collective-permute-start(bf16[512,256]{1,0:T(8,128)(2,1)S(1)} %select_convert_fusion.2), channel_id=1, source_target_pairs={{0,16},{1,17},{2,18},{3,19},{4,20},{5,21},{6,22},{7,23},{8,24},{9,... | collective-permute-start | bytes 786440 | tf_op jit(solution)/shard_map/ppermute | solution.py:15
  154.3 11.7 %collective-permute-done.4 = bf16[512,256]{1,0:T(8,128)(2,1)S(1)} collective-permute-done((bf16[512,256]{1,0:T(8,128)(2,1)S(1)}, bf16[512,256]{1,0:T(8,128)(2,1)S(1)}, u32[]{:S(2)}, u32[]{:S(2)}) %collective-permute-start.4) | collective-permute-done | bytes 262176 | tf_op jit(solution)/shard_map/ppermute | solution.py:15
  166.0 0.1 convert_add_fusion.2
  166.1 0.0 copy-start.2
  166.1 11.8 %collective-permute-start.5 = (bf16[512,128]{1,0:T(8,128)(2,1)S(1)}, bf16[512,128]{1,0:T(8,128)(2,1)S(1)}, u32[]{:S(2)}, u32[]{:S(2)}) collective-permute-start(bf16[512,128]{1,0:T(8,128)(2,1)S(1)} %select_convert_fusion.3), channel_id=1, source_target_pairs={{0,32},{1,33},{2,34},{3,35},{4,36},{5,37},{6,38},{7,39},{8,40},{9,... | collective-permute-start | bytes 393224 | tf_op jit(solution)/shard_map/ppermute | solution.py:15
  177.9 3.4 %collective-permute-done.5 = bf16[512,128]{1,0:T(8,128)(2,1)S(1)} collective-permute-done((bf16[512,128]{1,0:T(8,128)(2,1)S(1)}, bf16[512,128]{1,0:T(8,128)(2,1)S(1)}, u32[]{:S(2)}, u32[]{:S(2)}) %collective-permute-start.5) | collective-permute-done | bytes 131104 | tf_op jit(solution)/shard_map/ppermute | solution.py:15
  181.4 7.0 %collective-permute-start.6 = (bf16[512,128]{1,0:T(8,128)(2,1)S(1)}, bf16[512,128]{1,0:T(8,128)(2,1)S(1)}, u32[]{:S(2)}, u32[]{:S(2)}) collective-permute-start(bf16[512,128]{1,0:T(8,128)(2,1)S(1)} %add_convert_fusion), channel_id=1, source_target_pairs={{0,32},{1,33},{2,34},{3,35},{4,36},{5,37},{6,38},{7,39},{8,40},{9,... | collective-permute-start | bytes 393224 | tf_op jit(solution)/shard_map/ppermute | solution.py:15
  188.4 2.7 collective-permute-done.6
  191.1 0.1 maximum_select_fusion.14
  191.2 1.9 collective-permute-start.7
  193.1 10.6 %collective-permute-done.7 = bf16[512,256]{1,0:T(8,128)(2,1)S(1)} collective-permute-done((bf16[512,256]{1,0:T(8,128)(2,1)S(1)}, bf16[512,256]{1,0:T(8,128)(2,1)S(1)}, u32[]{:S(2)}, u32[]{:S(2)}) %collective-permute-start.7) | collective-permute-done | bytes 262176 | tf_op jit(solution)/shard_map/ppermute | solution.py:15
  203.7 0.1 maximum_select_fusion.9
  203.9 4.1 %collective-permute-start.8 = (bf16[512,512]{1,0:T(8,128)(2,1)S(1)}, bf16[512,512]{1,0:T(8,128)(2,1)S(1)}, u32[]{:S(2)}, u32[]{:S(2)}) collective-permute-start(bf16[512,512]{1,0:T(8,128)(2,1)S(1)} %maximum_select_fusion.9), channel_id=1, source_target_pairs={{0,8},{1,9},{2,10},{3,11},{4,12},{5,13},{6,14},{7,15},{8,0},{9,1},... | collective-permute-start | bytes 1572872 | tf_op jit(solution)/shard_map/ppermute | solution.py:15
  208.0 24.3 %collective-permute-done.8 = bf16[512,512]{1,0:T(8,128)(2,1)S(1)} collective-permute-done((bf16[512,512]{1,0:T(8,128)(2,1)S(1)}, bf16[512,512]{1,0:T(8,128)(2,1)S(1)}, u32[]{:S(2)}, u32[]{:S(2)}) %collective-permute-start.8) | collective-permute-done | bytes 524320 | tf_op jit(solution)/shard_map/ppermute | solution.py:15
  232.3 0.3 maximum_select_fusion.6
  232.6 1.9 collective-permute-start.9
  234.5 41.4 %collective-permute-done.9 = bf16[512,1024]{1,0:T(8,128)(2,1)S(1)} collective-permute-done((bf16[512,1024]{1,0:T(8,128)(2,1)S(1)}, bf16[512,1024]{1,0:T(8,128)(2,1)S(1)}, u32[]{:S(2)}, u32[]{:S(2)}) %collective-permute-start.9) | collective-permute-done | bytes 1048608 | tf_op jit(solution)/shard_map/ppermute | solution.py:15
  275.9 0.0 copy-done.2
  275.9 1.2 convolution_convert_fusion.1
  277.1 2.4 collective-permute-start.10
  279.5 1.4 collective-permute-done.10
  280.9 0.3 maximum_select_fusion.8
  281.2 1.9 collective-permute-start.11
  283.1 21.5 %collective-permute-done.11 = bf16[448,1024]{1,0:T(8,128)(2,1)S(1)} collective-permute-done((bf16[448,1024]{1,0:T(8,128)(2,1)S(1)}, bf16[448,1024]{1,0:T(8,128)(2,1)S(1)}, u32[]{:S(2)}, u32[]{:S(2)}) %collective-permute-start.11) | collective-permute-done | bytes 917536 | tf_op jit(solution)/shard_map/ppermute | solution.py:15
  304.6 2.0 fusion.8
  (3 shorter events, 0.1 us)
Async XLA Ops:
  23.3 12.0 %collective-permute-start = (bf16[112,2048]{1,0:T(8,128)(2,1)S(1)}, bf16[112,2048]{1,0:T(8,128)(2,1)S(1)}, u32[]{:S(2)}, u32[]{:S(2)}) collective-permute-start(bf16[112,2048]{1,0:T(8,128)(2,1)S(1)} %squeeze.3), channel_id=1, source_target_pairs={{0,1},{1,0},{2,3},{3,2},{4,5},{5,4},{6,7},{7,6},{8,9},{9,8},{10,11... | collective-permute-start | bytes 1376264 | tf_op jit(solution)/shard_map/ppermute | solution.py:15
  35.4 23.4 %collective-permute-start.1 = (bf16[224,2048]{1,0:T(8,128)(2,1)S(1)}, bf16[224,2048]{1,0:T(8,128)(2,1)S(1)}, u32[]{:S(2)}, u32[]{:S(2)}) collective-permute-start(bf16[224,2048]{1,0:T(8,128)(2,1)S(1)} %maximum_select_fusion.7), channel_id=1, source_target_pairs={{0,2},{1,3},{2,0},{3,1},{4,6},{5,7},{6,4},{7,5},{8,10},{9,11},{10,... | collective-permute-start | bytes 2752520 | tf_op jit(solution)/shard_map/ppermute | solution.py:15
  59.6 1.3 copy-start.1
  61.5 2.0 copy-start
  63.6 50.3 %collective-permute-start.2 = (bf16[512,1024]{1,0:T(8,128)(2,1)S(1)}, bf16[512,1024]{1,0:T(8,128)(2,1)S(1)}, u32[]{:S(2)}, u32[]{:S(2)}) collective-permute-start(bf16[512,1024]{1,0:T(8,128)(2,1)S(1)} %select_convert_fusion), channel_id=1, source_target_pairs={{0,4},{1,5},{2,6},{3,7},{4,0},{5,1},{6,2},{7,3},{8,12},{9,13},{10,... | collective-permute-start | bytes 3145736 | tf_op jit(solution)/shard_map/ppermute | solution.py:15
  116.9 30.6 %collective-permute-start.3 = (bf16[512,512]{1,0:T(8,128)(2,1)S(1)}, bf16[512,512]{1,0:T(8,128)(2,1)}, u32[]{:S(2)}, u32[]{:S(2)}) collective-permute-start(bf16[512,512]{1,0:T(8,128)(2,1)S(1)} %select_convert_fusion.1), channel_id=1, source_target_pairs={{0,8},{1,9},{2,10},{3,11},{4,12},{5,13},{6,14},{7,15},{8,0},{9,1},... | collective-permute-start | bytes 1572872 | tf_op jit(solution)/shard_map/ppermute | solution.py:15
  148.8 17.2 %collective-permute-start.4 = (bf16[512,256]{1,0:T(8,128)(2,1)S(1)}, bf16[512,256]{1,0:T(8,128)(2,1)S(1)}, u32[]{:S(2)}, u32[]{:S(2)}) collective-permute-start(bf16[512,256]{1,0:T(8,128)(2,1)S(1)} %select_convert_fusion.2), channel_id=1, source_target_pairs={{0,16},{1,17},{2,18},{3,19},{4,20},{5,21},{6,22},{7,23},{8,24},{9,... | collective-permute-start | bytes 786440 | tf_op jit(solution)/shard_map/ppermute | solution.py:15
  166.1 109.8 %copy-start.2 = (bf16[448,2048]{1,0:T(8,128)(2,1)S(1)}, bf16[448,2048]{1,0:T(8,128)(2,1)}, u32[]{:S(2)}) copy-start(bf16[448,2048]{1,0:T(8,128)(2,1)} %copy-done.1) | copy-start | bytes 5505028
  166.1 15.2 %collective-permute-start.5 = (bf16[512,128]{1,0:T(8,128)(2,1)S(1)}, bf16[512,128]{1,0:T(8,128)(2,1)S(1)}, u32[]{:S(2)}, u32[]{:S(2)}) collective-permute-start(bf16[512,128]{1,0:T(8,128)(2,1)S(1)} %select_convert_fusion.3), channel_id=1, source_target_pairs={{0,32},{1,33},{2,34},{3,35},{4,36},{5,37},{6,38},{7,39},{8,40},{9,... | collective-permute-start | bytes 393224 | tf_op jit(solution)/shard_map/ppermute | solution.py:15
  181.4 9.7 %collective-permute-start.6 = (bf16[512,128]{1,0:T(8,128)(2,1)S(1)}, bf16[512,128]{1,0:T(8,128)(2,1)S(1)}, u32[]{:S(2)}, u32[]{:S(2)}) collective-permute-start(bf16[512,128]{1,0:T(8,128)(2,1)S(1)} %add_convert_fusion), channel_id=1, source_target_pairs={{0,32},{1,33},{2,34},{3,35},{4,36},{5,37},{6,38},{7,39},{8,40},{9,... | collective-permute-start | bytes 393224 | tf_op jit(solution)/shard_map/ppermute | solution.py:15
  191.2 12.6 %collective-permute-start.7 = (bf16[512,256]{1,0:T(8,128)(2,1)S(1)}, bf16[512,256]{1,0:T(8,128)(2,1)S(1)}, u32[]{:S(2)}, u32[]{:S(2)}) collective-permute-start(bf16[512,256]{1,0:T(8,128)(2,1)S(1)} %maximum_select_fusion.14), channel_id=1, source_target_pairs={{0,16},{1,17},{2,18},{3,19},{4,20},{5,21},{6,22},{7,23},{8,24},{9,... | collective-permute-start | bytes 786440 | tf_op jit(solution)/shard_map/ppermute | solution.py:15
  203.9 28.4 %collective-permute-start.8 = (bf16[512,512]{1,0:T(8,128)(2,1)S(1)}, bf16[512,512]{1,0:T(8,128)(2,1)S(1)}, u32[]{:S(2)}, u32[]{:S(2)}) collective-permute-start(bf16[512,512]{1,0:T(8,128)(2,1)S(1)} %maximum_select_fusion.9), channel_id=1, source_target_pairs={{0,8},{1,9},{2,10},{3,11},{4,12},{5,13},{6,14},{7,15},{8,0},{9,1},... | collective-permute-start | bytes 1572872 | tf_op jit(solution)/shard_map/ppermute | solution.py:15
  232.6 43.3 %collective-permute-start.9 = (bf16[512,1024]{1,0:T(8,128)(2,1)S(1)}, bf16[512,1024]{1,0:T(8,128)(2,1)S(1)}, u32[]{:S(2)}, u32[]{:S(2)}) collective-permute-start(bf16[512,1024]{1,0:T(8,128)(2,1)S(1)} %maximum_select_fusion.6), channel_id=1, source_target_pairs={{0,4},{1,5},{2,6},{3,7},{4,0},{5,1},{6,2},{7,3},{8,12},{9,13},{10,... | collective-permute-start | bytes 3145736 | tf_op jit(solution)/shard_map/ppermute | solution.py:15
  277.1 3.8 %collective-permute-start.10 = (bf16[448,512]{1,0:T(8,128)(2,1)S(1)}, bf16[448,512]{1,0:T(8,128)(2,1)S(1)}, u32[]{:S(2)}, u32[]{:S(2)}) collective-permute-start(bf16[448,512]{1,0:T(8,128)(2,1)S(1)} %convolution_convert_fusion.1), channel_id=1, source_target_pairs={{0,1},{1,0},{2,3},{3,2},{4,5},{5,4},{6,7},{7,6},{8,9},{9,8},{10,11... | collective-permute-start | bytes 1376264 | tf_op jit(solution)/shard_map/ppermute | solution.py:15
  281.2 23.4 %collective-permute-start.11 = (bf16[448,1024]{1,0:T(8,128)(2,1)S(1)}, bf16[448,1024]{1,0:T(8,128)(2,1)S(1)}, u32[]{:S(2)}, u32[]{:S(2)}) collective-permute-start(bf16[448,1024]{1,0:T(8,128)(2,1)S(1)} %maximum_select_fusion.8), channel_id=1, source_target_pairs={{0,2},{1,3},{2,0},{3,1},{4,6},{5,7},{6,4},{7,5},{8,10},{9,11},{10,... | collective-permute-start | bytes 2752520 | tf_op jit(solution)/shard_map/ppermute | solution.py:15
where the time goes:
time: 307 us
  waiting for transfers between devices  213 us (69%)
  starting transfers between devices  56.7 us (18%)
  blocking collectives  21.8 us (7%)
  other arithmetic  6.81 us (2%)
  matrix products  4.49 us (1%)
  local copies, waits for them, and re-layouts  3.39 us (1%)
    ppermute x12, waiting for transfers between devices, partner(): return lax.ppermute(value, axis, pairs)  213 us
    ppermute x12, starting transfers between devices, partner(): return lax.ppermute(value, axis, pairs)  56.7 us
    all_to_all x1, blocking collectives, shards(): lax.all_to_all(iterate, 'expert', split_axis=0, concat_axis=1, tiled=True)  21.8 us
  transfers between devices with their start and end apart: 12, of which 12 were waited for; matrix products, arithmetic and copies ran while one was open for 0% of the time, Pallas kernels for 0%

commit v1 on v0

v1 whole, which is shorter than its diff:
```python
import functools
import math

import jax
import jax.numpy as jnp
from jax import lax
from jax.experimental import pallas as pl
from jax.experimental.pallas import tpu as pltpu
from jax.sharding import PartitionSpec as P

D = 7168
MOE_FF = 2048
N_Y = 8
N_Z = 4
SIDE = 128
STRIP = 9 * SIDE
PAIR = 10 * SIDE
WIDE = MOE_FF + PAIR
SCALE = 0.2 * math.sqrt(max(D, MOE_FF))
BF = jnp.bfloat16
F32 = jnp.float32


def block_pairs(shift_y, shift_z, flip):
    pairs = []
    for z in range(N_Z):
        for y in range(N_Y):
            for c in range(2):
                target = ((z + shift_z) % N_Z * N_Y + (y + shift_y) % N_Y) * 2 + (c ^ flip)
                pairs.append(((z * N_Y + y) * 2 + c, target))
    return pairs


def send(value, shift_y=0, shift_z=0, flip=0):
    return lax.ppermute(value, "block", block_pairs(shift_y, shift_z, flip))


def z_groups():
    return [[z * 16 + j for z in range(N_Z)] for j in range(16)]


def row_groups():
    return [[4 * p + q for q in range(4)] for p in range(16)]


def apply_kernel(where_ref, x_ref, *refs):
    mine, other = refs[:9], refs[9:18]
    out_ref, wide, acc, direct, turned = refs[18:]
    y, core = where_ref[0], where_ref[1]
    rows = x_ref.shape[0]

    def place(pieces, half):
        top = pl.multiple_of(half * SIDE, SIDE)
        for r in range(8):
            i = lax.rem(y + r, 8)
            if r < 4:
                parts = [(0, SIDE, pieces[r])]
            elif r == 4:
                parts = [(0, SIDE // 2, pieces[4]), (SIDE // 2, SIDE // 2, pieces[5])]
            else:
                parts = [(0, SIDE, pieces[r + 1])]
            for first, count, ref in parts:
                at = pl.ds(pl.multiple_of(top + first, 16), count)
                direct[i, at, pl.ds(top, STRIP)] = ref[...]
                turned[i, at, pl.ds(top, 7 * SIDE)] = ref[:, SIDE : 8 * SIDE]

    zero = jnp.zeros((SIDE, SIDE), BF)
    for i in range(8):
        direct[i, 0:SIDE, STRIP:PAIR] = zero
        direct[i, SIDE : 2 * SIDE, 0:SIDE] = zero
        turned[i, 0:SIDE, 7 * SIDE : 8 * SIDE] = zero
        turned[i, SIDE : 2 * SIDE, 0:SIDE] = zero
    place(mine, core)
    place(other, 1 - core)

    def times_gram(value):
        wide[:, 0:MOE_FF] = value
        wide[:, MOE_FF:WIDE] = value[:, 0:PAIR]
        acc[...] = jnp.zeros_like(acc)

        def step(i, carry):
            start = pl.multiple_of(i * 2 * SIDE, 2 * SIDE)
            acc[:, pl.ds(start, PAIR)] += lax.dot_general(
                wide[:, pl.ds(start, 2 * SIDE)], direct[i],
                (((1,), (0,)), ((), ())), preferred_element_type=F32,
            )
            acc[:, pl.ds(start, 2 * SIDE)] += lax.dot_general(
                wide[:, pl.ds(pl.multiple_of(start + SIDE, SIDE), 8 * SIDE)], turned[i],
                (((1,), (1,)), ((), ())), preferred_element_type=F32,
            )
            return carry

        lax.fori_loop(0, 8, step, 0)
        return jnp.concatenate(
            [acc[:, 0:PAIR] + acc[:, MOE_FF:WIDE], acc[:, PAIR:MOE_FF]], axis=1
        )

    x = x_ref[...]
    first = times_gram(x).astype(BF)
    second = times_gram(first)
    fresh = SCALE * (3.4445 * x.astype(F32) - 4.775 * first.astype(F32) + 2.0315 * second)
    fresh = fresh.astype(BF)
    for q in range(4):
        out_ref[q] = fresh[:, q * 512 : (q + 1) * 512]


def apply_gram(where, x, mine, other):
    rows = x.shape[0]
    vmem = pl.BlockSpec(memory_space=pltpu.VMEM)
    return pl.pallas_call(
        apply_kernel,
        out_shape=jax.ShapeDtypeStruct((4, rows, 512), BF),
        in_specs=[pl.BlockSpec(memory_space=pltpu.SMEM)] + [vmem] * 19,
        out_specs=vmem,
        scratch_shapes=[
            pltpu.VMEM((rows, WIDE), BF),
            pltpu.VMEM((rows, WIDE), F32),
            pltpu.VMEM((8, 2 * SIDE, PAIR), BF),
            pltpu.VMEM((8, 2 * SIDE, 8 * SIDE), BF),
        ],
        compiler_params=pltpu.CompilerParams(vmem_limit_bytes=40 * 2**20),
        cost_estimate=pl.CostEstimate(
            flops=4 * rows * MOE_FF * MOE_FF, bytes_accessed=5 * 2**20, transcendentals=0
        ),
    )(where, x, *mine, *other)


def shards(iterate):
    index = lax.axis_index("block")
    core = index % 2
    y = index // 2 % N_Y
    own = lax.all_to_all(iterate, "expert", split_axis=0, concat_axis=1, tiled=True)[0]
    both = jnp.concatenate([own, send(own, flip=1)], 0)
    ring = jnp.concatenate([both, both[:, : 8 * SIDE]], 1)

    def partial(d):
        at = (2 * ((y + d) % N_Y) + core) * SIDE
        left = lax.dynamic_slice_in_dim(ring, at, SIDE, 1)
        right = lax.dynamic_slice_in_dim(ring, at, STRIP, 1)
        return lax.dot_general(left, right, (((0,), (0,)), ((), ())), preferred_element_type=F32)

    half = SIDE // 2
    far = partial(4).astype(BF)
    up, down = far[:half], far[half:]
    for d in (3, 2, 1, 0):
        up, down = send(up, shift_y=1), send(down, shift_y=-1)
        if d == 3:
            a, b = partial(3), partial(-3)
            up = jnp.concatenate([a[:half] + up.astype(F32), a[half:]], 0).astype(BF)
            down = jnp.concatenate([b[:half], b[half:] + down.astype(F32)], 0).astype(BF)
        elif d:
            up = (partial(d) + up.astype(F32)).astype(BF)
            down = (partial(-d) + down.astype(F32)).astype(BF)
    summed = (partial(0) + up.astype(F32) + down.astype(F32)).astype(BF)
    parts = lax.all_to_all(summed, "block", 0, 0, axis_index_groups=z_groups(), tiled=True)
    parts = parts.reshape(N_Z, SIDE // N_Z, STRIP).astype(F32)
    piece = parts.sum(0).astype(BF)
    strip = lax.all_gather(piece, "block", axis=0, axis_index_groups=z_groups(), tiled=True)
    ups, downs = [strip], [strip]
    for d in range(1, 5):
        a, b = ups[-1], downs[-1]
        if d == 4:
            a, b = a[:half], b[half:]
        ups.append(send(a, shift_y=1))
        downs.append(send(b, shift_y=-1))
    mine = downs[:4] + [ups[4], downs[4], ups[3], ups[2], ups[1]]
    near = send(jnp.stack([strip, downs[1], downs[2], ups[2], ups[1]]), flip=1)
    far = send(jnp.concatenate([downs[3], ups[4], downs[4], ups[3]], 0), flip=1)
    other = [near[0], near[1], near[2], far[:SIDE], far[SIDE : SIDE + half], far[SIDE + half : 2 * SIDE], far[2 * SIDE :], near[3], near[4]]
    where = jnp.stack([y, core]).astype(jnp.int32)
    fresh = apply_gram(where, own, mine, other)
    out = lax.all_to_all(fresh, "block", 0, 1, axis_index_groups=row_groups(), tiled=True)
    return out[:, None]


def solution(mesh):
    return jax.shard_map(
        shards,
        mesh=mesh,
        in_specs=(P(None, ("expert", "block"), None),),
        out_specs=P("expert", "block", None, None),
        check_vma=False,
    )
```

time: 307 us -> 196 us (0.64)
  waiting for transfers between devices: 213 us -> 35 us
  blocking collectives: 21.8 us -> 67.7 us
  starting transfers between devices: 56.7 us -> 76.7 us
  Pallas kernels: 0 us -> 8.57 us
  other arithmetic: 6.81 us -> 0.3 us
    ppermute x12 -> x19, waiting for transfers between devices: 213 us -> 35 us  [send(): return lax.ppermute(value, 'block', block_pairs(shift_y, shift_z, flip))]
    all_to_all x0 -> x2, blocking collectives: none -> 33.4 us  [the longest x1 23.5 us: shards(): lax.all_to_all(summed, 'block', 0, 0, axis_index_groups=z_groups(), tiled...]
    ppermute x12 -> x19, starting transfers between devices: 56.7 us -> 76.7 us  [send(): return lax.ppermute(value, 'block', block_pairs(shift_y, shift_z, flip))]
    all_gather x0 -> x1, blocking collectives: none -> 12.5 us  [shards(): lax.all_gather(piece, 'block', axis=0, axis_index_groups=z_groups(), tile...]
    pallas_call x0 -> x1, Pallas kernels: none -> 8.57 us  [apply_gram(): pl.pallas_call(apply_kernel, out_shape=jax.ShapeDtypeStruct((4, rows, 512...]
    add x3 -> x0, other arithmetic: 4.19 us -> none  [shards(): summed = keep + incoming.astype(jnp.float32)]
  transfers between devices with their start and end apart: 12 -> 19, of which waited for: 12 -> 14; matrix products, arithmetic and copies ran while one was open for 0% -> 2% of each run, Pallas kernels for 0% -> 0%
where the time goes in v1:
time: 196 us; the launch traced here: 195 us
  starting transfers between devices  76.7 us (39%)
  blocking collectives  67.7 us (35%)
  waiting for transfers between devices  35 us (18%)
  Pallas kernels  8.57 us (4%)
  matrix products  3.29 us (2%)
  local copies, waits for them, and re-layouts  2.73 us (1%)
    ppermute x19, starting transfers between devices, send(): return lax.ppermute(value, 'block', block_pairs(shift_y, shift_z, flip))  76.7 us
    ppermute x19, waiting for transfers between devices, send(): return lax.ppermute(value, 'block', block_pairs(shift_y, shift_z, flip))  35 us
    all_to_all x1, blocking collectives, shards(): lax.all_to_all(summed, 'block', 0, 0, axis_index_groups=z_groups(), tiled...  23.5 us
    all_to_all x1, blocking collectives, shards(): lax.all_to_all(iterate, 'expert', split_axis=0, concat_axis=1, tiled=True)  21.8 us
    all_gather x1, blocking collectives, shards(): lax.all_gather(piece, 'block', axis=0, axis_index_groups=z_groups(), tile...  12.5 us
    all_to_all x1, blocking collectives, shards(): lax.all_to_all(fresh, 'block', 0, 1, axis_index_groups=row_groups(), tile...  9.88 us
    pallas_call x1, Pallas kernels, apply_gram(): pl.pallas_call(apply_kernel, out_shape=jax.ShapeDtypeStruct((4, rows, 512...  8.57 us
  transfers between devices with their start and end apart: 19, of which 14 were waited for; matrix products, arithmetic and copies ran while one was open for 2% of the time, Pallas kernels for 0%

profile of v1, /device:TPU:1, one launch (start us, length us, event | category | flops | bytes accessed | tf_op | source)
XLA Modules:
  0.0 195.0 jit_solution(12085926036893421255)
XLA Ops:
  0.0 1.3 copy.4
  1.3 21.8 %all_to_all.27 = bf16[16,7,2048]{2,1,0:T(8,128)(2,1)S(1)} all-to-all(bf16[16,7,2048]{2,1,0:T(8,128)(2,1)S(1)} %copy.4), channel_id=1, replica_groups=mesh['expert'=16,'block'=64] {'expert'}, dimensions={0} | all-to-all | bytes 917504 | tf_op jit(solution)/shard_map/all_to_all | solution.py:132
  23.3 10.5 %collective-permute-start = (bf16[112,2048]{1,0:T(8,128)(2,1)S(1)}, bf16[112,2048]{1,0:T(8,128)(2,1)S(1)}, u32[]{:S(2)}, u32[]{:S(2)}) collective-permute-start(bf16[112,2048]{1,0:T(8,128)(2,1)S(1)} %squeeze.18.x_ref), channel_id=1, source_target_pairs={{0,1},{1,0},{2,3},{3,2},{4,5},{5,4},{6,7},{7,6},{8,9},{9,8},{10,11... | collective-permute-start | bytes 1376264 | tf_op jit(solution)/shard_map/ppermute | solution.py:35
  33.9 1.3 collective-permute-done
  35.3 0.4 convolution_convert_fusion
  35.8 3.6 %collective-permute-start.5 = (bf16[64,1152]{1,0:T(8,128)(2,1)S(1)}, bf16[64,1152]{1,0:T(8,128)(2,1)S(1)}, u32[]{:S(2)}, u32[]{:S(2)}) collective-permute-start(bf16[64,1152]{1,0:T(8,128)(2,1)S(1)} %get-tuple-element.15), channel_id=1, source_target_pairs={{0,14},{1,15},{2,0},{3,1},{4,2},{5,3},{6,4},{7,5},{8,6},{9,7},{10,... | collective-permute-start | bytes 442376 | tf_op jit(solution)/shard_map/ppermute | solution.py:35
  39.4 0.4 fusion.7
  39.8 0.4 fusion.16
  40.3 1.9 collective-permute-start.1
  42.2 0.5 collective-permute-done.5
  42.7 4.9 %collective-permute-start.6 = (bf16[128,1152]{1,0:T(8,128)(2,1)S(1)}, bf16[128,1152]{1,0:T(8,128)(2,1)S(1)}, u32[]{:S(2)}, u32[]{:S(2)}) collective-permute-start(bf16[128,1152]{1,0:T(8,128)(2,1)S(1)} %pad_maximum_fusion.2), channel_id=1, source_target_pairs={{0,14},{1,15},{2,0},{3,1},{4,2},{5,3},{6,4},{7,5},{8,6},{9,7},{10,... | collective-permute-start | bytes 884744 | tf_op jit(solution)/shard_map/ppermute | solution.py:35
  47.6 0.5 collective-permute-done.1
  48.2 1.9 collective-permute-start.2
  50.2 2.5 %collective-permute-done.6 = bf16[128,1152]{1,0:T(8,128)(2,1)S(1)} collective-permute-done((bf16[128,1152]{1,0:T(8,128)(2,1)S(1)}, bf16[128,1152]{1,0:T(8,128)(2,1)S(1)}, u32[]{:S(2)}, u32[]{:S(2)}) %collective-permute-start.6) | collective-permute-done | bytes 294944 | tf_op jit(solution)/shard_map/ppermute | solution.py:35
  52.7 0.4 fusion.5
  53.1 5.3 %collective-permute-start.7 = (bf16[128,1152]{1,0:T(8,128)(2,1)S(1)}, bf16[128,1152]{1,0:T(8,128)(2,1)S(1)}, u32[]{:S(2)}, u32[]{:S(2)}) collective-permute-start(bf16[128,1152]{1,0:T(8,128)(2,1)S(1)} %fusion.5), channel_id=1, source_target_pairs={{0,14},{1,15},{2,0},{3,1},{4,2},{5,3},{6,4},{7,5},{8,6},{9,7},{10,... | collective-permute-start | bytes 884744 | tf_op jit(solution)/shard_map/ppermute | solution.py:35
  58.5 0.4 fusion.3
  58.9 1.9 collective-permute-start.3
  60.9 1.8 collective-permute-done.7
  62.7 0.4 fusion.4
  63.1 5.3 %collective-permute-start.8 = (bf16[128,1152]{1,0:T(8,128)(2,1)S(1)}, bf16[128,1152]{1,0:T(8,128)(2,1)S(1)}, u32[]{:S(2)}, u32[]{:S(2)}) collective-permute-start(bf16[128,1152]{1,0:T(8,128)(2,1)S(1)} %fusion.4), channel_id=1, source_target_pairs={{0,14},{1,15},{2,0},{3,1},{4,2},{5,3},{6,4},{7,5},{8,6},{9,7},{10,... | collective-permute-start | bytes 884744 | tf_op jit(solution)/shard_map/ppermute | solution.py:35
  68.5 0.4 fusion.2
  68.9 1.9 collective-permute-start.4
  70.8 1.3 collective-permute-done.8
  72.1 5.5 %collective-permute-done.4 = bf16[128,1152]{1,0:T(8,128)(2,1)S(1)} collective-permute-done((bf16[128,1152]{1,0:T(8,128)(2,1)S(1)}, bf16[128,1152]{1,0:T(8,128)(2,1)S(1)}, u32[]{:S(2)}, u32[]{:S(2)}) %collective-permute-start.4) | collective-permute-done | bytes 294944 | tf_op jit(solution)/shard_map/ppermute | solution.py:35
  77.6 0.4 fusion.1
  78.0 23.5 %all_to_all.28 = bf16[4,32,1152]{2,1,0:T(8,128)(2,1)S(1)} all-to-all(bf16[4,32,1152]{2,1,0:T(8,128)(2,1)S(1)} %bitcast.25), channel_id=1, replica_groups={{0,16,32,48},{1,17,33,49},{2,18,34,50},{3,19,35,51},{4,20,36,52},{5,21,..., dimensions={0} | all-to-all | bytes 589824 | tf_op jit(solution)/shard_map/all_to_all | solution.py:155
  101.6 12.5 %all_gather.3.refs_0_ = bf16[128,1152]{1,0:T(8,128)(2,1)S(1)} all-gather(bf16[32,1152]{1,0:T(8,128)(2,1)S(1)} %reduce_sum.12), channel_id=1, replica_groups={{0,16,32,48},{1,17,33,49},{2,18,34,50},{3,19,35,51},{4,20,36,52},{5,21,..., dimensions={0}, use_global_device_ids=true | all-gather | bytes 368640 | tf_op jit(solution)/shard_map/all_gather | solution.py:158
  114.1 1.9 collective-permute-start.9
  116.0 3.4 %collective-permute-start.12 = (bf16[128,1152]{1,0:T(8,128)(2,1)S(1)}, bf16[128,1152]{1,0:T(8,128)(2,1)S(1)}, u32[]{:S(2)}, u32[]{:S(2)}) collective-permute-start(bf16[128,1152]{1,0:T(8,128)(2,1)S(1)} %all_gather.3.refs_0_), channel_id=1, source_target_pairs={{0,2},{1,3},{2,4},{3,5},{4,6},{5,7},{6,8},{7,9},{8,10},{9,11},{10,... | collective-permute-start | bytes 884744 | tf_op jit(solution)/shard_map/ppermute | solution.py:35
  119.4 2.3 %collective-permute-done.9.refs_1_ = bf16[128,1152]{1,0:T(8,128)(2,1)S(1)} collective-permute-done((bf16[128,1152]{1,0:T(8,128)(2,1)S(1)}, bf16[128,1152]{1,0:T(8,128)(2,1)S(1)}, u32[]{:S(2)}, u32[]{:S(2)}) %collective-permute-start.9) | collective-permute-done | bytes 294944 | tf_op jit(solution)/shard_map/ppermute | solution.py:35
  121.7 3.0 %collective-permute-start.10 = (bf16[128,1152]{1,0:T(8,128)(2,1)S(1)}, bf16[128,1152]{1,0:T(8,128)(2,1)S(1)}, u32[]{:S(2)}, u32[]{:S(2)}) collective-permute-start(bf16[128,1152]{1,0:T(8,128)(2,1)S(1)} %collective-permute-done.9.refs_1_), channel_id=1, source_target_pairs={{0,14},{1,15},{2,0},{3,1},{4,2},{5,3},{6,4},{7,5},{8,6},{9,7},{10,... | collective-permute-start | bytes 884744 | tf_op jit(solution)/shard_map/ppermute | solution.py:35
  124.7 2.4 %collective-permute-start.13 = (bf16[128,1152]{1,0:T(8,128)(2,1)S(1)}, bf16[128,1152]{1,0:T(8,128)(2,1)S(1)}, u32[]{:S(2)}, u32[]{:S(2)}) collective-permute-start(bf16[128,1152]{1,0:T(8,128)(2,1)S(1)} %collective-permute-done.12.refs_8_), channel_id=1, source_target_pairs={{0,2},{1,3},{2,4},{3,5},{4,6},{5,7},{6,8},{7,9},{8,10},{9,11},{10,... | collective-permute-start | bytes 884744 | tf_op jit(solution)/shard_map/ppermute | solution.py:35
  127.1 4.6 %collective-permute-done.10.refs_2_ = bf16[128,1152]{1,0:T(8,128)(2,1)S(1)} collective-permute-done((bf16[128,1152]{1,0:T(8,128)(2,1)S(1)}, bf16[128,1152]{1,0:T(8,128)(2,1)S(1)}, u32[]{:S(2)}, u32[]{:S(2)}) %collective-permute-start.10) | collective-permute-done | bytes 294944 | tf_op jit(solution)/shard_map/ppermute | solution.py:35
  131.7 4.3 %collective-permute-start.11 = (bf16[128,1152]{1,0:T(8,128)(2,1)S(1)}, bf16[128,1152]{1,0:T(8,128)(2,1)S(1)}, u32[]{:S(2)}, u32[]{:S(2)}) collective-permute-start(bf16[128,1152]{1,0:T(8,128)(2,1)S(1)} %collective-permute-done.10.refs_2_), channel_id=1, source_target_pairs={{0,14},{1,15},{2,0},{3,1},{4,2},{5,3},{6,4},{7,5},{8,6},{9,7},{10,... | collective-permute-start | bytes 884744 | tf_op jit(solution)/shard_map/ppermute | solution.py:35
  136.0 0.4 collective-permute-done.13.refs_7_
  136.3 1.9 collective-permute-start.14
  138.3 9.3 %collective-permute-done.14.refs_6_ = bf16[128,1152]{1,0:T(8,128)(2,1)S(1)} collective-permute-done((bf16[128,1152]{1,0:T(8,128)(2,1)S(1)}, bf16[128,1152]{1,0:T(8,128)(2,1)S(1)}, u32[]{:S(2)}, u32[]{:S(2)}) %collective-permute-start.14) | collective-permute-done | bytes 294944 | tf_op jit(solution)/shard_map/ppermute | solution.py:35
  147.6 1.9 collective-permute-start.15
  149.6 4.6 %collective-permute-start.16 = (bf16[64,1152]{1,0:T(8,128)(2,1)S(1)}, bf16[64,1152]{1,0:T(8,128)(2,1)S(1)}, u32[]{:S(2)}, u32[]{:S(2)}) collective-permute-start(bf16[64,1152]{1,0:T(8,128)(2,1)S(1)} %slice.82), channel_id=1, source_target_pairs={{0,14},{1,15},{2,0},{3,1},{4,2},{5,3},{6,4},{7,5},{8,6},{9,7},{10,... | collective-permute-start | bytes 442376 | tf_op jit(solution)/shard_map/ppermute | solution.py:35
  154.2 0.5 collective-permute-done.15.refs_4_
  154.7 1.5 collective-permute-done.16.refs_5_
  156.3 14.1 %collective-permute-start.18 = (bf16[384,1152]{1,0:T(8,128)(2,1)S(1)}, bf16[384,1152]{1,0:T(8,128)(2,1)S(1)}, u32[]{:S(2)}, u32[]{:S(2)}) collective-permute-start(bf16[384,1152]{1,0:T(8,128)(2,1)S(1)} %pad_maximum_fusion), channel_id=1, source_target_pairs={{0,1},{1,0},{2,3},{3,2},{4,5},{5,4},{6,7},{7,6},{8,9},{9,8},{10,11... | collective-permute-start | bytes 2654216 | tf_op jit(solution)/shard_map/ppermute | solution.py:35
  170.5 1.9 collective-permute-start.17
  172.6 3.1 %collective-permute-done.17 = bf16[5,128,1152]{2,1,0:T(8,128)(2,1)S(1)} collective-permute-done((bf16[5,128,1152]{2,1,0:T(8,128)(2,1)S(1)}, bf16[5,128,1152]{2,1,0:T(8,128)(2,1)S(1)}, u32[]{:S(2)}, u32[]{:S(2)}) %collective-permute-start.17) | collective-permute-done | bytes 1474592 | tf_op jit(solution)/shard_map/ppermute | solution.py:35
  175.8 8.6 %shard_map.17 = bf16[4,112,512]{2,1,0:T(8,128)(2,1)S(1)} custom-call(s32[2]{0:T(128)S(1)} %pad_add_fusion.where_ref, bf16[112,2048]{1,0:T(8,128)(2,1)S(1)} %squeeze.18.x_ref, bf16[128,1152]{1,0:T(8,128)(2,1)S(1)} %all_gather.3.refs_0_, bf16[128,1152]{1,0:T(8,128)(2,1)S(1)} %collective-permute-done.9.refs_1_, ...), custom_call_target="tpu_custom_call" | custom-call | flops 1879048192 | bytes 5242880 | tf_op jit(solution)/shard_map/pallas_call | solution.py:110
  184.3 9.9 %all_to_all.29 = bf16[4,112,512]{2,1,0:T(8,128)(2,1)S(1)} all-to-all(bf16[4,112,512]{2,1,0:T(8,128)(2,1)S(1)} %shard_map.17), channel_id=1, replica_groups={{0,1,2,3},{4,5,6,7},{8,9,10,11},{12,13,14,15},{16,17,18,19},{20,21,22,2..., dimensions={0} | all-to-all | bytes 917504 | tf_op jit(solution)/shard_map/all_to_all | solution.py:172
  194.2 0.8 copy.11
  (29 shorter events, 1.0 us)
Async XLA Ops:
  23.3 12.0 %collective-permute-start = (bf16[112,2048]{1,0:T(8,128)(2,1)S(1)}, bf16[112,2048]{1,0:T(8,128)(2,1)S(1)}, u32[]{:S(2)}, u32[]{:S(2)}) collective-permute-start(bf16[112,2048]{1,0:T(8,128)(2,1)S(1)} %squeeze.18.x_ref), channel_id=1, source_target_pairs={{0,1},{1,0},{2,3},{3,2},{4,5},{5,4},{6,7},{7,6},{8,9},{9,8},{10,11... | collective-permute-start | bytes 1376264 | tf_op jit(solution)/shard_map/ppermute | solution.py:35
  35.8 6.9 %collective-permute-start.5 = (bf16[64,1152]{1,0:T(8,128)(2,1)S(1)}, bf16[64,1152]{1,0:T(8,128)(2,1)S(1)}, u32[]{:S(2)}, u32[]{:S(2)}) collective-permute-start(bf16[64,1152]{1,0:T(8,128)(2,1)S(1)} %get-tuple-element.15), channel_id=1, source_target_pairs={{0,14},{1,15},{2,0},{3,1},{4,2},{5,3},{6,4},{7,5},{8,6},{9,7},{10,... | collective-permute-start | bytes 442376 | tf_op jit(solution)/shard_map/ppermute | solution.py:35
  40.3 7.9 %collective-permute-start.1 = (bf16[64,1152]{1,0:T(8,128)(2,1)S(1)}, bf16[64,1152]{1,0:T(8,128)(2,1)S(1)}, u32[]{:S(2)}, u32[]{:S(2)}) collective-permute-start(bf16[64,1152]{1,0:T(8,128)(2,1)S(1)} %get-tuple-element.14), channel_id=1, source_target_pairs={{0,2},{1,3},{2,4},{3,5},{4,6},{5,7},{6,8},{7,9},{8,10},{9,11},{10,... | collective-permute-start | bytes 442376 | tf_op jit(solution)/shard_map/ppermute | solution.py:35
  42.7 10.0 %collective-permute-start.6 = (bf16[128,1152]{1,0:T(8,128)(2,1)S(1)}, bf16[128,1152]{1,0:T(8,128)(2,1)S(1)}, u32[]{:S(2)}, u32[]{:S(2)}) collective-permute-start(bf16[128,1152]{1,0:T(8,128)(2,1)S(1)} %pad_maximum_fusion.2), channel_id=1, source_target_pairs={{0,14},{1,15},{2,0},{3,1},{4,2},{5,3},{6,4},{7,5},{8,6},{9,7},{10,... | collective-permute-start | bytes 884744 | tf_op jit(solution)/shard_map/ppermute | solution.py:35
  48.2 10.2 %collective-permute-start.2 = (bf16[128,1152]{1,0:T(8,128)(2,1)S(1)}, bf16[128,1152]{1,0:T(8,128)(2,1)S(1)}, u32[]{:S(2)}, u32[]{:S(2)}) collective-permute-start(bf16[128,1152]{1,0:T(8,128)(2,1)S(1)} %pad_maximum_fusion.1), channel_id=1, source_target_pairs={{0,2},{1,3},{2,4},{3,5},{4,6},{5,7},{6,8},{7,9},{8,10},{9,11},{10,... | collective-permute-start | bytes 884744 | tf_op jit(solution)/shard_map/ppermute | solution.py:35
  53.1 9.6 %collective-permute-start.7 = (bf16[128,1152]{1,0:T(8,128)(2,1)S(1)}, bf16[128,1152]{1,0:T(8,128)(2,1)S(1)}, u32[]{:S(2)}, u32[]{:S(2)}) collective-permute-start(bf16[128,1152]{1,0:T(8,128)(2,1)S(1)} %fusion.5), channel_id=1, source_target_pairs={{0,14},{1,15},{2,0},{3,1},{4,2},{5,3},{6,4},{7,5},{8,6},{9,7},{10,... | collective-permute-start | bytes 884744 | tf_op jit(solution)/shard_map/ppermute | solution.py:35
  58.9 9.6 %collective-permute-start.3 = (bf16[128,1152]{1,0:T(8,128)(2,1)S(1)}, bf16[128,1152]{1,0:T(8,128)(2,1)S(1)}, u32[]{:S(2)}, u32[]{:S(2)}) collective-permute-start(bf16[128,1152]{1,0:T(8,128)(2,1)S(1)} %fusion.3), channel_id=1, source_target_pairs={{0,2},{1,3},{2,4},{3,5},{4,6},{5,7},{6,8},{7,9},{8,10},{9,11},{10,... | collective-permute-start | bytes 884744 | tf_op jit(solution)/shard_map/ppermute | solution.py:35
  63.1 9.0 %collective-permute-start.8 = (bf16[128,1152]{1,0:T(8,128)(2,1)S(1)}, bf16[128,1152]{1,0:T(8,128)(2,1)S(1)}, u32[]{:S(2)}, u32[]{:S(2)}) collective-permute-start(bf16[128,1152]{1,0:T(8,128)(2,1)S(1)} %fusion.4), channel_id=1, source_target_pairs={{0,14},{1,15},{2,0},{3,1},{4,2},{5,3},{6,4},{7,5},{8,6},{9,7},{10,... | collective-permute-start | bytes 884744 | tf_op jit(solution)/shard_map/ppermute | solution.py:35
  68.9 8.7 %collective-permute-start.4 = (bf16[128,1152]{1,0:T(8,128)(2,1)S(1)}, bf16[128,1152]{1,0:T(8,128)(2,1)S(1)}, u32[]{:S(2)}, u32[]{:S(2)}) collective-permute-start(bf16[128,1152]{1,0:T(8,128)(2,1)S(1)} %fusion.2), channel_id=1, source_target_pairs={{0,2},{1,3},{2,4},{3,5},{4,6},{5,7},{6,8},{7,9},{8,10},{9,11},{10,... | collective-permute-start | bytes 884744 | tf_op jit(solution)/shard_map/ppermute | solution.py:35
  114.1 7.6 %collective-permute-start.9 = (bf16[128,1152]{1,0:T(8,128)(2,1)S(1)}, bf16[128,1152]{1,0:T(8,128)(2,1)S(1)}, u32[]{:S(2)}, u32[]{:S(2)}) collective-permute-start(bf16[128,1152]{1,0:T(8,128)(2,1)S(1)} %all_gather.3.refs_0_), channel_id=1, source_target_pairs={{0,14},{1,15},{2,0},{3,1},{4,2},{5,3},{6,4},{7,5},{8,6},{9,7},{10,... | collective-permute-start | bytes 884744 | tf_op jit(solution)/shard_map/ppermute | solution.py:35
  116.0 8.7 %collective-permute-start.12 = (bf16[128,1152]{1,0:T(8,128)(2,1)S(1)}, bf16[128,1152]{1,0:T(8,128)(2,1)S(1)}, u32[]{:S(2)}, u32[]{:S(2)}) collective-permute-start(bf16[128,1152]{1,0:T(8,128)(2,1)S(1)} %all_gather.3.refs_0_), channel_id=1, source_target_pairs={{0,2},{1,3},{2,4},{3,5},{4,6},{5,7},{6,8},{7,9},{8,10},{9,11},{10,... | collective-permute-start | bytes 884744 | tf_op jit(solution)/shard_map/ppermute | solution.py:35
  121.7 10.0 %collective-permute-start.10 = (bf16[128,1152]{1,0:T(8,128)(2,1)S(1)}, bf16[128,1152]{1,0:T(8,128)(2,1)S(1)}, u32[]{:S(2)}, u32[]{:S(2)}) collective-permute-start(bf16[128,1152]{1,0:T(8,128)(2,1)S(1)} %collective-permute-done.9.refs_1_), channel_id=1, source_target_pairs={{0,14},{1,15},{2,0},{3,1},{4,2},{5,3},{6,4},{7,5},{8,6},{9,7},{10,... | collective-permute-start | bytes 884744 | tf_op jit(solution)/shard_map/ppermute | solution.py:35
  124.7 11.7 %collective-permute-start.13 = (bf16[128,1152]{1,0:T(8,128)(2,1)S(1)}, bf16[128,1152]{1,0:T(8,128)(2,1)S(1)}, u32[]{:S(2)}, u32[]{:S(2)}) collective-permute-start(bf16[128,1152]{1,0:T(8,128)(2,1)S(1)} %collective-permute-done.12.refs_8_), channel_id=1, source_target_pairs={{0,2},{1,3},{2,4},{3,5},{4,6},{5,7},{6,8},{7,9},{8,10},{9,11},{10,... | collective-permute-start | bytes 884744 | tf_op jit(solution)/shard_map/ppermute | solution.py:35
  131.7 17.8 %collective-permute-start.11 = (bf16[128,1152]{1,0:T(8,128)(2,1)S(1)}, bf16[128,1152]{1,0:T(8,128)(2,1)S(1)}, u32[]{:S(2)}, u32[]{:S(2)}) collective-permute-start(bf16[128,1152]{1,0:T(8,128)(2,1)S(1)} %collective-permute-done.10.refs_2_), channel_id=1, source_target_pairs={{0,14},{1,15},{2,0},{3,1},{4,2},{5,3},{6,4},{7,5},{8,6},{9,7},{10,... | collective-permute-start | bytes 884744 | tf_op jit(solution)/shard_map/ppermute | solution.py:35
  136.3 11.3 %collective-permute-start.14 = (bf16[128,1152]{1,0:T(8,128)(2,1)S(1)}, bf16[128,1152]{1,0:T(8,128)(2,1)S(1)}, u32[]{:S(2)}, u32[]{:S(2)}) collective-permute-start(bf16[128,1152]{1,0:T(8,128)(2,1)S(1)} %collective-permute-done.13.refs_7_), channel_id=1, source_target_pairs={{0,2},{1,3},{2,4},{3,5},{4,6},{5,7},{6,8},{7,9},{8,10},{9,11},{10,... | collective-permute-start | bytes 884744 | tf_op jit(solution)/shard_map/ppermute | solution.py:35
  147.6 7.1 %collective-permute-start.15 = (bf16[64,1152]{1,0:T(8,128)(2,1)S(1)}, bf16[64,1152]{1,0:T(8,128)(2,1)S(1)}, u32[]{:S(2)}, u32[]{:S(2)}) collective-permute-start(bf16[64,1152]{1,0:T(8,128)(2,1)S(1)} %slice.81), channel_id=1, source_target_pairs={{0,2},{1,3},{2,4},{3,5},{4,6},{5,7},{6,8},{7,9},{8,10},{9,11},{10,... | collective-permute-start | bytes 442376 | tf_op jit(solution)/shard_map/ppermute | solution.py:35
  149.6 6.7 %collective-permute-start.16 = (bf16[64,1152]{1,0:T(8,128)(2,1)S(1)}, bf16[64,1152]{1,0:T(8,128)(2,1)S(1)}, u32[]{:S(2)}, u32[]{:S(2)}) collective-permute-start(bf16[64,1152]{1,0:T(8,128)(2,1)S(1)} %slice.82), channel_id=1, source_target_pairs={{0,14},{1,15},{2,0},{3,1},{4,2},{5,3},{6,4},{7,5},{8,6},{9,7},{10,... | collective-permute-start | bytes 442376 | tf_op jit(solution)/shard_map/ppermute | solution.py:35
  156.3 16.2 %collective-permute-start.18 = (bf16[384,1152]{1,0:T(8,128)(2,1)S(1)}, bf16[384,1152]{1,0:T(8,128)(2,1)S(1)}, u32[]{:S(2)}, u32[]{:S(2)}) collective-permute-start(bf16[384,1152]{1,0:T(8,128)(2,1)S(1)} %pad_maximum_fusion), channel_id=1, source_target_pairs={{0,1},{1,0},{2,3},{3,2},{4,5},{5,4},{6,7},{7,6},{8,9},{9,8},{10,11... | collective-permute-start | bytes 2654216 | tf_op jit(solution)/shard_map/ppermute | solution.py:35
  170.5 5.2 %collective-permute-start.17 = (bf16[5,128,1152]{2,1,0:T(8,128)(2,1)S(1)}, bf16[5,128,1152]{2,1,0:T(8,128)(2,1)S(1)}, u32[]{:S(2)}, u32[]{:S(2)}) collective-permute-start(bf16[5,128,1152]{2,1,0:T(8,128)(2,1)S(1)} %bitcast_dynamic-update-slice_fusion), channel_id=1, source_target_pairs={{0,1},{1,0},{2,3},{3,2},{4,5},{5,4},{6,7},{7,6},{8,9},{9,8},{10,11... | collective-permute-start | bytes 4423688 | tf_op jit(solution)/shard_map/ppermute | solution.py:35

commit v2 on v1

v2 whole, which is shorter than its diff:
```python
import math

import jax
import jax.numpy as jnp
from jax import lax
from jax.experimental import pallas as pl
from jax.experimental.pallas import tpu as pltpu
from jax.sharding import PartitionSpec as P

D = 7168
MOE_FF = 2048
N_Y = 8
N_Z = 4
SIDE = 128
SLAB = SIDE // N_Z
STRIP = 9 * SIDE
PAIR = 10 * SIDE
WIDE = MOE_FF + PAIR
SCALE = 0.2 * math.sqrt(max(D, MOE_FF))
BF = jnp.bfloat16
F32 = jnp.float32


def swap_cores(value):
    return lax.ppermute(value, "block", [(i, i ^ 1) for i in range(2 * N_Y * N_Z)])


def core_groups():
    return [[2 * i + c for i in range(N_Y * N_Z)] for c in range(2)]


def row_groups():
    return [[4 * p + q for q in range(4)] for p in range(16)]


def strips_kernel(core_ref, own_ref, other_ref, out_ref, wide):
    rows = own_ref.shape[0]
    for first, ref in ((0, own_ref), (rows, other_ref)):
        wide[first : first + rows, 0:MOE_FF] = ref[...]
        wide[first : first + rows, MOE_FF : MOE_FF + 8 * SIDE] = ref[:, 0 : 8 * SIDE]

    def strip(y, carry):
        start = pl.multiple_of((2 * y + core_ref[0]) * SIDE, SIDE)
        value = lax.dot_general(
            wide[:, pl.ds(start, SIDE)], wide[:, pl.ds(start, STRIP)],
            (((0,), (0,)), ((), ())), preferred_element_type=F32,
        ).astype(BF)
        for z in range(N_Z):
            out_ref[z, y] = value[z * SLAB : (z + 1) * SLAB]
        return carry

    lax.fori_loop(0, N_Y, strip, 0)


def make_strips(core, own, other):
    vmem = pl.BlockSpec(memory_space=pltpu.VMEM)
    rows = own.shape[0]
    return pl.pallas_call(
        strips_kernel,
        out_shape=jax.ShapeDtypeStruct((N_Z, N_Y, SLAB, STRIP), BF),
        in_specs=[pl.BlockSpec(memory_space=pltpu.SMEM), vmem, vmem],
        out_specs=vmem,
        scratch_shapes=[pltpu.VMEM((2 * rows, MOE_FF + 8 * SIDE), BF)],
        compiler_params=pltpu.CompilerParams(vmem_limit_bytes=32 * 2**20),
        cost_estimate=pl.CostEstimate(
            flops=4 * rows * SIDE * STRIP * N_Y, bytes_accessed=4 * 2**20, transcendentals=0
        ),
    )(core, own, other)


def apply_kernel(core_ref, x_ref, mine_ref, other_ref, out_ref, wide, acc, direct, turned):
    zero = jnp.zeros((SIDE, SIDE), BF)
    for ref, half in ((mine_ref, core_ref[0]), (other_ref, 1 - core_ref[0])):
        top = pl.multiple_of(half * SIDE, SIDE)
        for y in range(N_Y):
            for z in range(N_Z):
                at = pl.ds(pl.multiple_of(top + z * SLAB, SLAB), SLAB)
                direct[y, at, pl.ds(top, STRIP)] = ref[z, y]
                turned[y, at, pl.ds(top, 7 * SIDE)] = ref[z, y, :, SIDE : 8 * SIDE]
    for i in range(N_Y):
        direct[i, 0:SIDE, STRIP:PAIR] = zero
        direct[i, SIDE : 2 * SIDE, 0:SIDE] = zero
        turned[i, 0:SIDE, 7 * SIDE : 8 * SIDE] = zero
        turned[i, SIDE : 2 * SIDE, 0:SIDE] = zero

    def times_gram(value):
        wide[:, 0:MOE_FF] = value
        wide[:, MOE_FF:WIDE] = value[:, 0:PAIR]
        acc[...] = jnp.zeros_like(acc)

        def step(i, carry):
            start = pl.multiple_of(i * 2 * SIDE, 2 * SIDE)
            acc[:, pl.ds(start, PAIR)] += lax.dot_general(
                wide[:, pl.ds(start, 2 * SIDE)], direct[i],
                (((1,), (0,)), ((), ())), preferred_element_type=F32,
            )
            acc[:, pl.ds(start, 2 * SIDE)] += lax.dot_general(
                wide[:, pl.ds(pl.multiple_of(start + SIDE, SIDE), 8 * SIDE)], turned[i],
                (((1,), (1,)), ((), ())), preferred_element_type=F32,
            )
            return carry

        lax.fori_loop(0, N_Y, step, 0)
        return jnp.concatenate(
            [acc[:, 0:PAIR] + acc[:, MOE_FF:WIDE], acc[:, PAIR:MOE_FF]], axis=1
        )

    x = x_ref[...]
    first = times_gram(x).astype(BF)
    second = times_gram(first)
    fresh = SCALE * (3.4445 * x.astype(F32) - 4.775 * first.astype(F32) + 2.0315 * second)
    fresh = fresh.astype(BF)
    for q in range(4):
        out_ref[q] = fresh[:, q * 512 : (q + 1) * 512]


def apply_gram(core, x, mine, other):
    rows = x.shape[0]
    vmem = pl.BlockSpec(memory_space=pltpu.VMEM)
    return pl.pallas_call(
        apply_kernel,
        out_shape=jax.ShapeDtypeStruct((4, rows, 512), BF),
        in_specs=[pl.BlockSpec(memory_space=pltpu.SMEM)] + [vmem] * 3,
        out_specs=vmem,
        scratch_shapes=[
            pltpu.VMEM((rows, WIDE), BF),
            pltpu.VMEM((rows, WIDE), F32),
            pltpu.VMEM((N_Y, 2 * SIDE, PAIR), BF),
            pltpu.VMEM((N_Y, 2 * SIDE, 8 * SIDE), BF),
        ],
        compiler_params=pltpu.CompilerParams(vmem_limit_bytes=40 * 2**20),
        cost_estimate=pl.CostEstimate(
            flops=4 * rows * MOE_FF * MOE_FF, bytes_accessed=5 * 2**20, transcendentals=0
        ),
    )(core, x, mine, other)


def shards(iterate):
    index = lax.axis_index("block")
    core = (index % 2).astype(jnp.int32)[None]
    own = lax.all_to_all(iterate, "expert", split_axis=0, concat_axis=1, tiled=True)[0]
    strips = make_strips(core, own, swap_cores(own))
    groups = core_groups()
    count = N_Y * N_Z
    strips = strips.reshape(count, SLAB, STRIP)
    parts = lax.all_to_all(strips, "block", 0, 0, axis_index_groups=groups, tiled=True)
    piece = parts.astype(F32).sum(0).astype(BF)
    copies = jnp.broadcast_to(piece[None], (count, SLAB, STRIP))
    mine = lax.all_to_all(copies, "block", 0, 0, axis_index_groups=groups, tiled=True)
    mine = mine.reshape(N_Z, N_Y, SLAB, STRIP)
    fresh = apply_gram(core, own, mine, swap_cores(mine))
    out = lax.all_to_all(fresh, "block", 0, 1, axis_index_groups=row_groups(), tiled=True)
    return out[:, None]


def solution(mesh):
    return jax.shard_map(
        shards,
        mesh=mesh,
        in_specs=(P(None, ("expert", "block"), None),),
        out_specs=P("expert", "block", None, None),
        check_vma=False,
    )
```

time: 196 us -> 209 us (1.066)
  blocking collectives: 67.7 us -> 174 us
  starting transfers between devices: 76.7 us -> 15.8 us
  waiting for transfers between devices: 35 us -> 5.55 us
  matrix products: 3.29 us -> 0 us
    all_to_all x1 -> x2, blocking collectives: 23.5 us -> 142 us  [the longest x1 76.2 us: shards(): lax.all_to_all(strips, 'block', 0, 0, axis_index_groups=groups, tiled=True)]
    ppermute x19 -> x2, starting transfers between devices: 76.7 us -> 15.8 us  [swap_cores(): lax.ppermute(value, 'block', [(i, i ^ 1) for i in range(2 * N_Y * N_Z)])]
    ppermute x19 -> x2, waiting for transfers between devices: 35 us -> 5.55 us  [swap_cores(): lax.ppermute(value, 'block', [(i, i ^ 1) for i in range(2 * N_Y * N_Z)])]
    all_gather x1 -> x0, blocking collectives: 12.5 us -> none  [shards(): lax.all_gather(piece, 'block', axis=0, axis_index_groups=z_groups(), tile...]
    dot_general x8 -> x0, matrix products: 3.29 us -> none  [partial(): lax.dot_general(left, right, (((0,), (0,)), ((), ())), preferred_element_...]
    pallas_call x0 -> x1, Pallas kernels: none -> 2.31 us  [make_strips(): pl.pallas_call(strips_kernel, out_shape=jax.ShapeDtypeStruct((N_Z, N_Y, S...]
  transfers between devices with their start and end apart: 19 -> 2, of which waited for: 14 -> 2; matrix products, arithmetic and copies ran while one was open for 2% -> 0% of each run, Pallas kernels for 0% -> 0%
where the time goes in v2:
time: 209 us; the launch traced here: 208 us
  blocking collectives  174 us (83%)
  starting transfers between devices  15.8 us (8%)
  Pallas kernels  10.3 us (5%)
  waiting for transfers between devices  5.55 us (3%)
  local copies, waits for them, and re-layouts  2.37 us (1%)
    all_to_all x1, blocking collectives, shards(): lax.all_to_all(strips, 'block', 0, 0, axis_index_groups=groups, tiled=True)  76.2 us
    all_to_all x1, blocking collectives, shards(): lax.all_to_all(copies, 'block', 0, 0, axis_index_groups=groups, tiled=True)  65.3 us
    all_to_all x1, blocking collectives, shards(): lax.all_to_all(iterate, 'expert', split_axis=0, concat_axis=1, tiled=True)  21.8 us
    ppermute x2, starting transfers between devices, swap_cores(): lax.ppermute(value, 'block', [(i, i ^ 1) for i in range(2 * N_Y * N_Z)])  15.8 us
    all_to_all x1, blocking collectives, shards(): lax.all_to_all(fresh, 'block', 0, 1, axis_index_groups=row_groups(), tile...  10.4 us
    pallas_call x1, Pallas kernels, apply_gram(): pl.pallas_call(apply_kernel, out_shape=jax.ShapeDtypeStruct((4, rows, 512...  8 us
    ppermute x2, waiting for transfers between devices, swap_cores(): lax.ppermute(value, 'block', [(i, i ^ 1) for i in range(2 * N_Y * N_Z)])  5.55 us
  transfers between devices with their start and end apart: 2, of which 2 were waited for; matrix products, arithmetic and copies ran while one was open for 0% of the time, Pallas kernels for 0%

profile of v2, /device:TPU:1, one launch (start us, length us, event | category | flops | bytes accessed | tf_op | source)
XLA Modules:
  0.0 208.3 jit_solution(4055128393582504973)
XLA Ops:
  0.0 1.3 copy.4
  1.3 21.8 %all_to_all.28 = bf16[16,7,2048]{2,1,0:T(8,128)(2,1)S(1)} all-to-all(bf16[16,7,2048]{2,1,0:T(8,128)(2,1)S(1)} %copy.4), channel_id=1, replica_groups=mesh['expert'=16,'block'=64] {'expert'}, dimensions={0} | all-to-all | bytes 917504 | tf_op jit(solution)/shard_map/all_to_all | solution.py:141
  23.1 0.2 squeeze.3.own_ref.x_ref
  23.3 10.5 %collective-permute-start = (bf16[112,2048]{1,0:T(8,128)(2,1)S(1)}, bf16[112,2048]{1,0:T(8,128)(2,1)S(1)}, u32[]{:S(2)}, u32[]{:S(2)}) collective-permute-start(bf16[112,2048]{1,0:T(8,128)(2,1)S(1)} %squeeze.3.own_ref.x_ref), channel_id=1, source_target_pairs={{0,1},{1,0},{2,3},{3,2},{4,5},{5,4},{6,7},{7,6},{8,9},{9,8},{10,11... | collective-permute-start | bytes 1376264 | tf_op jit(solution)/shard_map/ppermute | solution.py:25
  33.8 1.4 collective-permute-done.other_ref
  35.2 2.3 %shard_map.17 = bf16[4,8,32,1152]{3,2,1,0:T(8,128)(2,1)S(1)} custom-call(s32[1]{0:T(128)} %bitcast.core_ref, bf16[112,2048]{1,0:T(8,128)(2,1)S(1)} %squeeze.3.own_ref.x_ref, bf16[112,2048]{1,0:T(8,128)(2,1)S(1)} %collective-permute-done.other_ref), custom_call_target="tpu_custom_call" | custom-call | flops 528482304 | bytes 4194304 | tf_op jit(solution)/shard_map/pallas_call | solution.py:58
  37.5 76.2 %all_to_all.29 = bf16[32,32,1152]{2,1,0:T(8,128)(2,1)S(1)} all-to-all(bf16[32,32,1152]{2,1,0:T(8,128)(2,1)S(1)} %bitcast.4), channel_id=1, replica_groups={{0,2,4,6,8,10,12,14,16,18,20,22,24,26,28,30,32,34,36,38,40,42,44,46,48,..., dimensions={0} | all-to-all | bytes 4718592 | tf_op jit(solution)/shard_map/all_to_all | solution.py:146
  113.8 0.3 reduce_sum.12
  114.1 0.2 broadcast_in_dim.13
  114.3 65.3 %all_to_all.30 = bf16[32,32,1152]{2,1,0:T(8,128)(2,1)S(1)} all-to-all(bf16[32,32,1152]{2,1,0:T(8,128)(2,1)S(1)} %broadcast_in_dim.13), channel_id=1, replica_groups={{0,2,4,6,8,10,12,14,16,18,20,22,24,26,28,30,32,34,36,38,40,42,44,46,48,..., dimensions={0} | all-to-all | bytes 4718592 | tf_op jit(solution)/shard_map/all_to_all | solution.py:149
  179.6 5.3 %collective-permute-start.1 = (bf16[4,8,32,1152]{3,2,1,0:T(8,128)(2,1)S(1)}, bf16[4,8,32,1152]{3,2,1,0:T(8,128)(2,1)S(1)}, u32[]{:S(2)}, u32[]{:S(2)}) collective-permute-start(bf16[4,8,32,1152]{3,2,1,0:T(8,128)(2,1)S(1)} %bitcast.5), channel_id=1, source_target_pairs={{0,1},{1,0},{2,3},{3,2},{4,5},{5,4},{6,7},{7,6},{8,9},{9,8},{10,11... | collective-permute-start | bytes 7077896 | tf_op jit(solution)/shard_map/ppermute | solution.py:25
  184.9 4.1 %collective-permute-done.1.other_ref = bf16[4,8,32,1152]{3,2,1,0:T(8,128)(2,1)S(1)} collective-permute-done((bf16[4,8,32,1152]{3,2,1,0:T(8,128)(2,1)S(1)}, bf16[4,8,32,1152]{3,2,1,0:T(8,128)(2,1)S(1)}, u32[]{:S(2)}, u32[]{:S(2)}) %collective-permute-start.1) | collective-permute-done | bytes 2359328 | tf_op jit(solution)/shard_map/ppermute | solution.py:25
  189.1 8.0 %shard_map.18 = bf16[4,112,512]{2,1,0:T(8,128)(2,1)S(1)} custom-call(s32[1]{0:T(128)} %bitcast.core_ref, bf16[112,2048]{1,0:T(8,128)(2,1)S(1)} %squeeze.3.own_ref.x_ref, bf16[4,8,32,1152]{3,2,1,0:T(8,128)(2,1)S(1)} %bitcast.6, bf16[4,8,32,1152]{3,2,1,0:T(8,128)(2,1)S(1)} %collective-permute-done.1.other_ref), custom_call_target="tpu_custom_call" | custom-call | flops 1879048192 | bytes 5242880 | tf_op jit(solution)/shard_map/pallas_call | solution.py:120
  197.1 10.4 %all_to_all.31 = bf16[4,112,512]{2,1,0:T(8,128)(2,1)S(1)} all-to-all(bf16[4,112,512]{2,1,0:T(8,128)(2,1)S(1)} %shard_map.18), channel_id=1, replica_groups={{0,1,2,3},{4,5,6,7},{8,9,10,11},{12,13,14,15},{16,17,18,19},{20,21,22,2..., dimensions={0} | all-to-all | bytes 917504 | tf_op jit(solution)/shard_map/all_to_all | solution.py:152
  207.5 0.8 copy.6
Async XLA Ops:
  23.3 12.0 %collective-permute-start = (bf16[112,2048]{1,0:T(8,128)(2,1)S(1)}, bf16[112,2048]{1,0:T(8,128)(2,1)S(1)}, u32[]{:S(2)}, u32[]{:S(2)}) collective-permute-start(bf16[112,2048]{1,0:T(8,128)(2,1)S(1)} %squeeze.3.own_ref.x_ref), channel_id=1, source_target_pairs={{0,1},{1,0},{2,3},{3,2},{4,5},{5,4},{6,7},{7,6},{8,9},{9,8},{10,11... | collective-permute-start | bytes 1376264 | tf_op jit(solution)/shard_map/ppermute | solution.py:25
  179.6 9.4 %collective-permute-start.1 = (bf16[4,8,32,1152]{3,2,1,0:T(8,128)(2,1)S(1)}, bf16[4,8,32,1152]{3,2,1,0:T(8,128)(2,1)S(1)}, u32[]{:S(2)}, u32[]{:S(2)}) collective-permute-start(bf16[4,8,32,1152]{3,2,1,0:T(8,128)(2,1)S(1)} %bitcast.5), channel_id=1, source_target_pairs={{0,1},{1,0},{2,3},{3,2},{4,5},{5,4},{6,7},{7,6},{8,9},{9,8},{10,11... | collective-permute-start | bytes 7077896 | tf_op jit(solution)/shard_map/ppermute | solution.py:25

commit v3 on v2

--- a/solution.py
+++ b/solution.py
@@ -5,6 +5,7 @@
 from jax import lax
 from jax.experimental import pallas as pl
 from jax.experimental.pallas import tpu as pltpu
+from jax.sharding import Mesh
 from jax.sharding import PartitionSpec as P
 
 D = 7168
@@ -22,25 +23,24 @@
 
 
 def swap_cores(value):
-    return lax.ppermute(value, "block", [(i, i ^ 1) for i in range(2 * N_Y * N_Z)])
+    return lax.ppermute(value, "c", [(0, 1), (1, 0)])
 
 
-def core_groups():
-    return [[2 * i + c for i in range(N_Y * N_Z)] for c in range(2)]
+def send_y(value, shift):
+    return lax.ppermute(value, ("yh", "yl"), [(y, (y + shift) % N_Y) for y in range(N_Y)])
 
 
-def row_groups():
-    return [[4 * p + q for q in range(4)] for p in range(16)]
-
-
-def strips_kernel(core_ref, own_ref, other_ref, out_ref, wide):
-    rows = own_ref.shape[0]
-    for first, ref in ((0, own_ref), (rows, other_ref)):
-        wide[first : first + rows, 0:MOE_FF] = ref[...]
-        wide[first : first + rows, MOE_FF : MOE_FF + 8 * SIDE] = ref[:, 0 : 8 * SIDE]
+def strips_kernel(first_ref, *refs):
+    out_ref, wide = refs[-2:]
+    at = 0
+    for ref in refs[:-2]:
+        rows = ref.shape[0]
+        wide[at : at + rows, 0:MOE_FF] = ref[...]
+        wide[at : at + rows, MOE_FF : MOE_FF + 8 * SIDE] = ref[:, 0 : 8 * SIDE]
+        at += rows
 
     def strip(y, carry):
-        start = pl.multiple_of((2 * y + core_ref[0]) * SIDE, SIDE)
+        start = pl.multiple_of((4 * y + first_ref[0]) * SIDE, SIDE)
         value = lax.dot_general(
             wide[:, pl.ds(start, SIDE)], wide[:, pl.ds(start, STRIP)],
             (((0,), (0,)), ((), ())), preferred_element_type=F32,
@@ -49,23 +49,23 @@
             out_ref[z, y] = value[z * SLAB : (z + 1) * SLAB]
         return carry
 
-    lax.fori_loop(0, N_Y, strip, 0)
+    lax.fori_loop(0, N_Y // 2, strip, 0)
 
 
-def make_strips(core, own, other):
+def make_strips(first, pieces):
     vmem = pl.BlockSpec(memory_space=pltpu.VMEM)
-    rows = own.shape[0]
+    rows = sum(piece.shape[0] for piece in pieces)
     return pl.pallas_call(
         strips_kernel,
-        out_shape=jax.ShapeDtypeStruct((N_Z, N_Y, SLAB, STRIP), BF),
-        in_specs=[pl.BlockSpec(memory_space=pltpu.SMEM), vmem, vmem],
+        out_shape=jax.ShapeDtypeStruct((N_Z, N_Y // 2, SLAB, STRIP), BF),
+        in_specs=[pl.BlockSpec(memory_space=pltpu.SMEM)] + [vmem] * len(pieces),
         out_specs=vmem,
-        scratch_shapes=[pltpu.VMEM((2 * rows, MOE_FF + 8 * SIDE), BF)],
+        scratch_shapes=[pltpu.VMEM((rows, MOE_FF + 8 * SIDE), BF)],
         compiler_params=pltpu.CompilerParams(vmem_limit_bytes=32 * 2**20),
         cost_estimate=pl.CostEstimate(
-            flops=4 * rows * SIDE * STRIP * N_Y, bytes_accessed=4 * 2**20, transcendentals=0
+            flops=rows * SIDE * STRIP * N_Y, bytes_accessed=4 * 2**20, transcendentals=0
         ),
-    )(core, own, other)
+    )(first, *pieces)
 
 
 def apply_kernel(core_ref, x_ref, mine_ref, other_ref, out_ref, wide, acc, direct, turned):
@@ -136,28 +136,31 @@
 
 
 def shards(iterate):
-    index = lax.axis_index("block")
-    core = (index % 2).astype(jnp.int32)[None]
-    own = lax.all_to_all(iterate, "expert", split_axis=0, concat_axis=1, tiled=True)[0]
-    strips = make_strips(core, own, swap_cores(own))
-    groups = core_groups()
-    count = N_Y * N_Z
-    strips = strips.reshape(count, SLAB, STRIP)
-    parts = lax.all_to_all(strips, "block", 0, 0, axis_index_groups=groups, tiled=True)
+    core = lax.axis_index("c").astype(jnp.int32)
+    parity = lax.axis_index("yl").astype(jnp.int32)
+    own = lax.all_to_all(iterate, ("x", "zl"), split_axis=0, concat_axis=1, tiled=True)[0]
+    half = own.shape[0] // 2
+    near = jnp.concatenate([send_y(own[:half], 1), send_y(own[half:], -1)], 0)
+    pieces = [own, swap_cores(own), near, swap_cores(near)]
+    strips = make_strips((2 * parity + core)[None], pieces)
+    strips = strips.reshape(N_Z * N_Y // 2, SLAB, STRIP)
+    parts = lax.all_to_all(strips, ("zh", "yh"), 0, 0, tiled=True)
     piece = parts.astype(F32).sum(0).astype(BF)
-    copies = jnp.broadcast_to(piece[None], (count, SLAB, STRIP))
-    mine = lax.all_to_all(copies, "block", 0, 0, axis_index_groups=groups, tiled=True)
+    copies = jnp.broadcast_to(piece[None], (N_Z * N_Y, SLAB, STRIP))
+    mine = lax.all_to_all(copies, ("zh", "yh", "yl"), 0, 0, tiled=True)
     mine = mine.reshape(N_Z, N_Y, SLAB, STRIP)
-    fresh = apply_gram(core, own, mine, swap_cores(mine))
-    out = lax.all_to_all(fresh, "block", 0, 1, axis_index_groups=row_groups(), tiled=True)
+    fresh = apply_gram(core[None], own, mine, swap_cores(mine))
+    out = lax.all_to_all(fresh, ("yl", "c"), 0, 1, tiled=True)
     return out[:, None]
 
 
 def solution(mesh):
+    names = ("x", "zl", "zh", "yh", "yl", "c")
+    split = Mesh(mesh.devices.reshape(8, 2, N_Z, N_Y // 2, 2, 2), names)
     return jax.shard_map(
         shards,
-        mesh=mesh,
-        in_specs=(P(None, ("expert", "block"), None),),
-        out_specs=P("expert", "block", None, None),
+        mesh=split,
+        in_specs=(P(None, names, None),),
+        out_specs=P(names[:2], names[2:], None, None),
         check_vma=False,
     )

time: 209 us -> 193 us (0.923)
  blocking collectives: 174 us -> 148 us
  starting transfers between devices: 15.8 us -> 26.9 us
    all_to_all x4, blocking collectives: 174 us -> 148 us  [the longest x1 68.4 us: shards(): mine = lax.all_to_all(copies, ('zh', 'yh', 'yl'), 0, 0, tiled=True)]
    ppermute x2 -> x5, starting transfers between devices: 15.8 us -> 26.9 us  [the longest x3 15.3 us: swap_cores(): return lax.ppermute(value, 'c', [(0, 1), (1, 0)])]
    ppermute x2 -> x5, waiting for transfers between devices: 5.55 us -> 5.55 us  [the longest x3 5.54 us: swap_cores(): return lax.ppermute(value, 'c', [(0, 1), (1, 0)])]
  transfers between devices with their start and end apart: 2 -> 5, of which waited for: 2 -> 2; matrix products, arithmetic and copies ran while one was open for 0% -> 0% of each run, Pallas kernels for 0% -> 0%
where the time goes in v3:
time: 193 us
  blocking collectives  148 us (77%)
  starting transfers between devices  26.9 us (14%)
  Pallas kernels  9.65 us (5%)
  waiting for transfers between devices  5.55 us (3%)
  local copies, waits for them, and re-layouts  2.62 us (1%)
    all_to_all x1, blocking collectives, shards(): mine = lax.all_to_all(copies, ('zh', 'yh', 'yl'), 0, 0, tiled=True)  68.4 us
    all_to_all x1, blocking collectives, shards(): parts = lax.all_to_all(strips, ('zh', 'yh'), 0, 0, tiled=True)  47.4 us
    all_to_all x1, blocking collectives, shards(): lax.all_to_all(iterate, ('x', 'zl'), split_axis=0, concat_axis=1, tiled=T...  21.8 us
    ppermute x3, starting transfers between devices, swap_cores(): return lax.ppermute(value, 'c', [(0, 1), (1, 0)])  15.3 us
    ppermute x2, starting transfers between devices, send_y(): lax.ppermute(value, ('yh', 'yl'), [(y, (y + shift) % N_Y) for y in range(...  11.6 us
    all_to_all x1, blocking collectives, shards(): out = lax.all_to_all(fresh, ('yl', 'c'), 0, 1, tiled=True)  10.1 us
    pallas_call x1, Pallas kernels, apply_gram(): pl.pallas_call(apply_kernel, out_shape=jax.ShapeDtypeStruct((4, rows, 512...  8 us
    ppermute x3, waiting for transfers between devices, swap_cores(): return lax.ppermute(value, 'c', [(0, 1), (1, 0)])  5.54 us
  transfers between devices with their start and end apart: 5, of which 2 were waited for; matrix products, arithmetic and copies ran while one was open for 0% of the time, Pallas kernels for 0%

profile of v3, /device:TPU:1, one launch (start us, length us, event | category | flops | bytes accessed | tf_op | source)
XLA Modules:
  0.0 192.8 jit_solution(16136551255011048413)
XLA Ops:
  0.0 1.3 copy.8
  1.3 21.8 %all_to_all.28 = bf16[16,7,2048]{2,1,0:T(8,128)(2,1)S(1)} all-to-all(bf16[16,7,2048]{2,1,0:T(8,128)(2,1)S(1)} %copy.8), channel_id=1, replica_groups=mesh['x'=8,'zl'=2,'zh'=4,'yh'=4,'yl'=2,'c'=2] {'x','zl'}, dimensions={0} | all-to-all | bytes 917504 | tf_op jit(solution)/shard_map/all_to_all | solution.py:141
  23.1 0.1 slice.13
  23.2 7.1 %collective-permute-start.1 = (bf16[56,2048]{1,0:T(8,128)(2,1)S(1)}, bf16[56,2048]{1,0:T(8,128)(2,1)S(1)}, u32[]{:S(2)}, u32[]{:S(2)}) collective-permute-start(bf16[56,2048]{1,0:T(8,128)(2,1)S(1)} %slice.13), channel_id=1, source_target_pairs={{0,2},{2,4},{4,6},{6,8},{8,10},{10,12},{12,14},{14,0},{1,3},{3,5},... | collective-permute-start | bytes 688136 | tf_op jit(solution)/shard_map/ppermute | solution.py:30
  30.4 0.1 slice.15
  30.5 4.5 %collective-permute-start.2 = (bf16[56,2048]{1,0:T(8,128)(2,1)S(1)}, bf16[56,2048]{1,0:T(8,128)(2,1)S(1)}, u32[]{:S(2)}, u32[]{:S(2)}) collective-permute-start(bf16[56,2048]{1,0:T(8,128)(2,1)S(1)} %slice.15), channel_id=1, source_target_pairs={{0,14},{2,0},{4,2},{6,4},{8,6},{10,8},{12,10},{14,12},{1,15},{3,1}... | collective-permute-start | bytes 688136 | tf_op jit(solution)/shard_map/ppermute | solution.py:30
  35.0 0.2 squeeze.3.refs_0_.x_ref
  35.1 6.0 %collective-permute-start = (bf16[112,2048]{1,0:T(8,128)(2,1)S(1)}, bf16[112,2048]{1,0:T(8,128)(2,1)S(1)}, u32[]{:S(2)}, u32[]{:S(2)}) collective-permute-start(bf16[112,2048]{1,0:T(8,128)(2,1)S(1)} %squeeze.3.refs_0_.x_ref), channel_id=1, source_target_pairs={{0,1},{1,0},{2,3},{3,2},{4,5},{5,4},{6,7},{7,6},{8,9},{9,8},{10,11... | collective-permute-start | bytes 1376264 | tf_op jit(solution)/shard_map/ppermute | solution.py:26
  41.1 0.0 collective-permute-done.1
  41.1 0.0 collective-permute-done.2
  41.2 3.3 %collective-permute-start.3 = (bf16[112,2048]{1,0:T(8,128)(2,1)S(1)}, bf16[112,2048]{1,0:T(8,128)(2,1)S(1)}, u32[]{:S(2)}, u32[]{:S(2)}) collective-permute-start(bf16[112,2048]{1,0:T(8,128)(2,1)S(1)} %constant_dynamic-update-slice_fusion.refs_2_), channel_id=1, source_target_pairs={{0,1},{1,0},{2,3},{3,2},{4,5},{5,4},{6,7},{7,6},{8,9},{9,8},{10,11... | collective-permute-start | bytes 1376264 | tf_op jit(solution)/shard_map/ppermute | solution.py:26
  44.5 0.0 collective-permute-done.refs_1_
  44.5 1.4 collective-permute-done.3.refs_3_
  45.9 1.7 shard_map.17
  47.6 47.4 %all_to_all.29 = bf16[16,32,1152]{2,1,0:T(8,128)(2,1)S(1)} all-to-all(bf16[16,32,1152]{2,1,0:T(8,128)(2,1)S(1)} %bitcast.5), channel_id=1, replica_groups=mesh['x'=8,'zl'=2,'zh'=4,'yh'=4,'yl'=2,'c'=2] {'zh','yh'}, dimensions={0} | all-to-all | bytes 2359296 | tf_op jit(solution)/shard_map/all_to_all | solution.py:147
  95.0 0.2 reduce_sum.12
  95.2 0.2 broadcast_in_dim.17
  95.3 68.4 %all_to_all.30 = bf16[32,32,1152]{2,1,0:T(8,128)(2,1)S(1)} all-to-all(bf16[32,32,1152]{2,1,0:T(8,128)(2,1)S(1)} %broadcast_in_dim.17), channel_id=1, replica_groups=mesh['x'=8,'zl'=2,'zh'=4,'yh'=4,'yl'=2,'c'=2] {'zh','yh','yl'}, dimensions={0} | all-to-all | bytes 4718592 | tf_op jit(solution)/shard_map/all_to_all | solution.py:150
  163.7 6.0 %collective-permute-start.4 = (bf16[4,8,32,1152]{3,2,1,0:T(8,128)(2,1)S(1)}, bf16[4,8,32,1152]{3,2,1,0:T(8,128)(2,1)S(1)}, u32[]{:S(2)}, u32[]{:S(2)}) collective-permute-start(bf16[4,8,32,1152]{3,2,1,0:T(8,128)(2,1)S(1)} %bitcast.6), channel_id=1, source_target_pairs={{0,1},{1,0},{2,3},{3,2},{4,5},{5,4},{6,7},{7,6},{8,9},{9,8},{10,11... | collective-permute-start | bytes 7077896 | tf_op jit(solution)/shard_map/ppermute | solution.py:26
  169.8 4.1 %collective-permute-done.4.other_ref = bf16[4,8,32,1152]{3,2,1,0:T(8,128)(2,1)S(1)} collective-permute-done((bf16[4,8,32,1152]{3,2,1,0:T(8,128)(2,1)S(1)}, bf16[4,8,32,1152]{3,2,1,0:T(8,128)(2,1)S(1)}, u32[]{:S(2)}, u32[]{:S(2)}) %collective-permute-start.4) | collective-permute-done | bytes 2359328 | tf_op jit(solution)/shard_map/ppermute | solution.py:26
  173.9 8.0 %shard_map.18 = bf16[4,112,512]{2,1,0:T(8,128)(2,1)S(1)} custom-call(s32[1]{0:T(128)} %bitcast.core_ref, bf16[112,2048]{1,0:T(8,128)(2,1)S(1)} %squeeze.3.refs_0_.x_ref, bf16[4,8,32,1152]{3,2,1,0:T(8,128)(2,1)S(1)} %bitcast.7, bf16[4,8,32,1152]{3,2,1,0:T(8,128)(2,1)S(1)} %collective-permute-done.4.other_ref), custom_call_target="tpu_custom_call" | custom-call | flops 1879048192 | bytes 5242880 | tf_op jit(solution)/shard_map/pallas_call | solution.py:120
  181.9 10.1 %all_to_all.31 = bf16[4,112,512]{2,1,0:T(8,128)(2,1)S(1)} all-to-all(bf16[4,112,512]{2,1,0:T(8,128)(2,1)S(1)} %shard_map.18), channel_id=1, replica_groups=mesh['x'=8,'zl'=2,'zh'=4,'yh'=4,'yl'=2,'c'=2] {'yl','c'}, dimensions={0} | all-to-all | bytes 917504 | tf_op jit(solution)/shard_map/all_to_all | solution.py:153
  192.0 0.8 copy.11
  (3 shorter events, 0.1 us)
Async XLA Ops:
  23.2 17.9 %collective-permute-start.1 = (bf16[56,2048]{1,0:T(8,128)(2,1)S(1)}, bf16[56,2048]{1,0:T(8,128)(2,1)S(1)}, u32[]{:S(2)}, u32[]{:S(2)}) collective-permute-start(bf16[56,2048]{1,0:T(8,128)(2,1)S(1)} %slice.13), channel_id=1, source_target_pairs={{0,2},{2,4},{4,6},{6,8},{8,10},{10,12},{12,14},{14,0},{1,3},{3,5},... | collective-permute-start | bytes 688136 | tf_op jit(solution)/shard_map/ppermute | solution.py:30
  30.5 10.7 %collective-permute-start.2 = (bf16[56,2048]{1,0:T(8,128)(2,1)S(1)}, bf16[56,2048]{1,0:T(8,128)(2,1)S(1)}, u32[]{:S(2)}, u32[]{:S(2)}) collective-permute-start(bf16[56,2048]{1,0:T(8,128)(2,1)S(1)} %slice.15), channel_id=1, source_target_pairs={{0,14},{2,0},{4,2},{6,4},{8,6},{10,8},{12,10},{14,12},{1,15},{3,1}... | collective-permute-start | bytes 688136 | tf_op jit(solution)/shard_map/ppermute | solution.py:30
  35.1 9.4 %collective-permute-start = (bf16[112,2048]{1,0:T(8,128)(2,1)S(1)}, bf16[112,2048]{1,0:T(8,128)(2,1)S(1)}, u32[]{:S(2)}, u32[]{:S(2)}) collective-permute-start(bf16[112,2048]{1,0:T(8,128)(2,1)S(1)} %squeeze.3.refs_0_.x_ref), channel_id=1, source_target_pairs={{0,1},{1,0},{2,3},{3,2},{4,5},{5,4},{6,7},{7,6},{8,9},{9,8},{10,11... | collective-permute-start | bytes 1376264 | tf_op jit(solution)/shard_map/ppermute | solution.py:26
  41.2 4.7 %collective-permute-start.3 = (bf16[112,2048]{1,0:T(8,128)(2,1)S(1)}, bf16[112,2048]{1,0:T(8,128)(2,1)S(1)}, u32[]{:S(2)}, u32[]{:S(2)}) collective-permute-start(bf16[112,2048]{1,0:T(8,128)(2,1)S(1)} %constant_dynamic-update-slice_fusion.refs_2_), channel_id=1, source_target_pairs={{0,1},{1,0},{2,3},{3,2},{4,5},{5,4},{6,7},{7,6},{8,9},{9,8},{10,11... | collective-permute-start | bytes 1376264 | tf_op jit(solution)/shard_map/ppermute | solution.py:26
  163.7 10.2 %collective-permute-start.4 = (bf16[4,8,32,1152]{3,2,1,0:T(8,128)(2,1)S(1)}, bf16[4,8,32,1152]{3,2,1,0:T(8,128)(2,1)S(1)}, u32[]{:S(2)}, u32[]{:S(2)}) collective-permute-start(bf16[4,8,32,1152]{3,2,1,0:T(8,128)(2,1)S(1)} %bitcast.6), channel_id=1, source_target_pairs={{0,1},{1,0},{2,3},{3,2},{4,5},{5,4},{6,7},{7,6},{8,9},{9,8},{10,11... | collective-permute-start | bytes 7077896 | tf_op jit(solution)/shard_map/ppermute | solution.py:26

commit v4 on v2

v4 whole, which is shorter than its diff:
```python
import functools
import math

import jax
import jax.numpy as jnp
from jax import lax
from jax.experimental import pallas as pl
from jax.experimental.pallas import tpu as pltpu
from jax.sharding import Mesh
from jax.sharding import PartitionSpec as P

D = 7168
MOE_FF = 2048
N_Y = 8
N_Z = 4
SIDE = 128
SLAB = SIDE // N_Z
STRIP = 8 * SIDE
PAIR = 10 * SIDE
TURN = 9 * SIDE
EXTRA = SIDE // 2 // N_Z
PIECE = 8 * SLAB + EXTRA
WIDE = MOE_FF + PAIR
SCALE = 0.2 * math.sqrt(max(D, MOE_FF))
BF = jnp.bfloat16
F32 = jnp.float32


def swap_cores(value):
    return lax.ppermute(value, "c", [(0, 1), (1, 0)])


def strips_kernel(core_ref, own_ref, other_ref, out_ref, wide):
    rows = own_ref.shape[0]
    for first, ref in ((0, own_ref), (rows, other_ref)):
        wide[first : first + rows, 0:MOE_FF] = ref[...]
        wide[first : first + rows, MOE_FF : MOE_FF + 8 * SIDE] = ref[:, 0 : 8 * SIDE]

    def times(left, right, width):
        return lax.dot_general(
            wide[:, pl.ds(pl.multiple_of(left, SIDE), SIDE)],
            wide[:, pl.ds(pl.multiple_of(right, SIDE), width)],
            (((0,), (0,)), ((), ())), preferred_element_type=F32,
        )

    def strip(y, carry):
        start = (2 * y + core_ref[0]) * SIDE
        value = times(start, start, STRIP).astype(BF)
        low = (2 * lax.rem(y, 4) + core_ref[0]) * SIDE
        extra = times(low, low + 8 * SIDE, SIDE)
        extra = jnp.where(y < 4, extra[: SIDE // 2], extra[SIDE // 2 :]).astype(BF)
        for z in range(N_Z):
            for m in range(8):
                out_ref[z, y, m * SLAB : (m + 1) * SLAB] = value[
                    z * SLAB : (z + 1) * SLAB, m * SIDE : (m + 1) * SIDE
                ]
            out_ref[z, y, 8 * SLAB : PIECE] = extra[z * EXTRA : (z + 1) * EXTRA]
        return carry

    lax.fori_loop(0, N_Y, strip, 0)


def make_strips(core, own, other):
    vmem = pl.BlockSpec(memory_space=pltpu.VMEM)
    rows = own.shape[0]
    return pl.pallas_call(
        strips_kernel,
        out_shape=jax.ShapeDtypeStruct((N_Z, N_Y, PIECE, SIDE), BF),
        in_specs=[pl.BlockSpec(memory_space=pltpu.SMEM), vmem, vmem],
        out_specs=vmem,
        scratch_shapes=[pltpu.VMEM((2 * rows, MOE_FF + 8 * SIDE), BF)],
        compiler_params=pltpu.CompilerParams(vmem_limit_bytes=32 * 2**20),
        cost_estimate=pl.CostEstimate(
            flops=4 * rows * SIDE * TURN * N_Y, bytes_accessed=4 * 2**20, transcendentals=0
        ),
    )(core, own, other)


def apply_kernel(core_ref, x_ref, mine_ref, other_ref, out_ref, wide, acc, direct, turned):
    for ref, half in ((mine_ref, core_ref[0]), (other_ref, 1 - core_ref[0])):
        top = pl.multiple_of(half * SIDE, SIDE)

        def block(m):
            return pl.ds(pl.multiple_of(top + m * SIDE, SIDE), SIDE)

        for y in range(N_Y):
            for z in range(N_Z):
                at = pl.ds(pl.multiple_of(top + z * SLAB, SLAB), SLAB)
                for m in range(8):
                    value = ref[z, y, m * SLAB : (m + 1) * SLAB]
                    direct[y, at, block(m)] = value
                    if m:
                        turned[y, at, block(m - 1)] = value
                first = top + z * EXTRA + y // 4 * (SIDE // 2)
                at = pl.ds(pl.multiple_of(first, EXTRA), EXTRA)
                value = ref[z, y, 8 * SLAB : PIECE]
                direct[y % 4, at, block(8)] = value
                turned[y % 4, at, block(7)] = value
    zero = jnp.zeros((SIDE, SIDE), BF)
    for i in range(N_Y):
        last = 9 if i < 4 else 8
        direct[i, 0:SIDE, last * SIDE : (last + 1) * SIDE] = zero
        direct[i, SIDE : 2 * SIDE, 0:SIDE] = zero
        turned[i, 0:SIDE, (last - 1) * SIDE : last * SIDE] = zero
        turned[i, SIDE : 2 * SIDE, 0:SIDE] = zero

    def times_gram(value):
        wide[:, 0:MOE_FF] = value
        wide[:, MOE_FF:WIDE] = value[:, 0:PAIR]
        acc[...] = jnp.zeros_like(acc)

        def step(width, i, carry):
            start = pl.multiple_of(i * 2 * SIDE, 2 * SIDE)
            acc[:, pl.ds(start, width)] += lax.dot_general(
                wide[:, pl.ds(start, 2 * SIDE)], direct[i, :, 0:width],
                (((1,), (0,)), ((), ())), preferred_element_type=F32,
            )
            acc[:, pl.ds(start, 2 * SIDE)] += lax.dot_general(
                wide[:, pl.ds(pl.multiple_of(start + SIDE, SIDE), width - SIDE)],
                turned[i, :, 0 : width - SIDE],
                (((1,), (1,)), ((), ())), preferred_element_type=F32,
            )
            return carry

        lax.fori_loop(0, 4, functools.partial(step, PAIR), 0)
        lax.fori_loop(4, N_Y, functools.partial(step, TURN), 0)
        return jnp.concatenate(
            [acc[:, 0:PAIR] + acc[:, MOE_FF:WIDE], acc[:, PAIR:MOE_FF]], axis=1
        )

    x = x_ref[...]
    first = times_gram(x).astype(BF)
    second = times_gram(first)
    fresh = SCALE * (3.4445 * x.astype(F32) - 4.775 * first.astype(F32) + 2.0315 * second)
    fresh = fresh.astype(BF)
    for q in range(4):
        out_ref[q] = fresh[:, q * 512 : (q + 1) * 512]


def apply_gram(core, x, mine, other):
    rows = x.shape[0]
    vmem = pl.BlockSpec(memory_space=pltpu.VMEM)
    return pl.pallas_call(
        apply_kernel,
        out_shape=jax.ShapeDtypeStruct((4, rows, 512), BF),
        in_specs=[pl.BlockSpec(memory_space=pltpu.SMEM)] + [vmem] * 3,
        out_specs=vmem,
        scratch_shapes=[
            pltpu.VMEM((rows, WIDE), BF),
            pltpu.VMEM((rows, WIDE), F32),
            pltpu.VMEM((N_Y, 2 * SIDE, PAIR), BF),
            pltpu.VMEM((N_Y, 2 * SIDE, TURN), BF),
        ],
        compiler_params=pltpu.CompilerParams(vmem_limit_bytes=40 * 2**20),
        cost_estimate=pl.CostEstimate(
            flops=4 * rows * MOE_FF * MOE_FF, bytes_accessed=5 * 2**20, transcendentals=0
        ),
    )(core, x, mine, other)


def exchange(value):
    groups = [[4 * p + q for q in range(4)] for p in range(N_Y // 2)]
    return lax.all_to_all(value, ("y", "c"), 0, 1, axis_index_groups=groups, tiled=True)


def shards(iterate):
    core = lax.axis_index("c").astype(jnp.int32)[None]
    own = lax.all_to_all(iterate, ("x", "zl"), split_axis=0, concat_axis=1, tiled=True)[0]
    strips = make_strips(core, own, swap_cores(own))
    count = N_Y * N_Z
    strips = strips.reshape(count, PIECE, SIDE)
    parts = lax.all_to_all(strips, ("zh", "y"), 0, 0, tiled=True)
    piece = parts.astype(F32).sum(0).astype(BF)
    copies = jnp.broadcast_to(piece[None], (count, PIECE, SIDE))
    mine = lax.all_to_all(copies, ("zh", "y"), 0, 0, tiled=True)
    mine = mine.reshape(N_Z, N_Y, PIECE, SIDE)
    fresh = apply_gram(core, own, mine, swap_cores(mine))
    return exchange(fresh)[:, None]


def solution(mesh):
    names = ("x", "zl", "zh", "y", "c")
    split = Mesh(mesh.devices.reshape(8, 2, N_Z, N_Y, 2), names)
    return jax.shard_map(
        shards,
        mesh=split,
        in_specs=(P(None, names, None),),
        out_specs=P(names[:2], names[2:], None, None),
        check_vma=False,
    )
```

time: 209 us -> 204 us (0.976)
  blocking collectives: 174 us -> 169 us
    all_to_all x4, blocking collectives: 174 us -> 169 us  [the longest x1 75.3 us: shards(): parts = lax.all_to_all(strips, ('zh', 'y'), 0, 0, tiled=True)]
where the time goes in v4:
time: 204 us
  blocking collectives  169 us (83%)
  starting transfers between devices  15 us (7%)
  Pallas kernels  11.1 us (5%)
  waiting for transfers between devices  5.37 us (3%)
  local copies, waits for them, and re-layouts  2.49 us (1%)
    all_to_all x1, blocking collectives, shards(): parts = lax.all_to_all(strips, ('zh', 'y'), 0, 0, tiled=True)  75.3 us
    all_to_all x1, blocking collectives, shards(): mine = lax.all_to_all(copies, ('zh', 'y'), 0, 0, tiled=True)  62.1 us
    all_to_all x1, blocking collectives, shards(): lax.all_to_all(iterate, ('x', 'zl'), split_axis=0, concat_axis=1, tiled=T...  21.8 us
    ppermute x2, starting transfers between devices, swap_cores(): return lax.ppermute(value, 'c', [(0, 1), (1, 0)])  15 us
    all_to_all x1, blocking collectives, exchange(): lax.all_to_all(value, ('y', 'c'), 0, 1, axis_index_groups=groups, tiled=T...  10.1 us
    pallas_call x1, Pallas kernels, apply_gram(): pl.pallas_call(apply_kernel, out_shape=jax.ShapeDtypeStruct((4, rows, 512...  8.74 us
    ppermute x2, waiting for transfers between devices, swap_cores(): return lax.ppermute(value, 'c', [(0, 1), (1, 0)])  5.37 us
  transfers between devices with their start and end apart: 2, of which 2 were waited for; matrix products, arithmetic and copies ran while one was open for 0% of the time, Pallas kernels for 0%

profile of v4, /device:TPU:1, one launch (start us, length us, event | category | flops | bytes accessed | tf_op | source)
XLA Modules:
  0.0 203.7 jit_solution(17262963462434338351)
XLA Ops:
  0.0 1.3 copy.4
  1.3 21.8 %all_to_all.28 = bf16[16,7,2048]{2,1,0:T(8,128)(2,1)S(1)} all-to-all(bf16[16,7,2048]{2,1,0:T(8,128)(2,1)S(1)} %copy.4), channel_id=1, replica_groups=mesh['x'=8,'zl'=2,'zh'=4,'y'=8,'c'=2] {'x','zl'}, dimensions={0} | all-to-all | bytes 917504 | tf_op jit(solution)/shard_map/all_to_all | solution.py:168
  23.1 0.2 squeeze.3.own_ref.x_ref
  23.3 10.5 %collective-permute-start = (bf16[112,2048]{1,0:T(8,128)(2,1)S(1)}, bf16[112,2048]{1,0:T(8,128)(2,1)S(1)}, u32[]{:S(2)}, u32[]{:S(2)}) collective-permute-start(bf16[112,2048]{1,0:T(8,128)(2,1)S(1)} %squeeze.3.own_ref.x_ref), channel_id=1, source_target_pairs={{0,1},{1,0},{2,3},{3,2},{4,5},{5,4},{6,7},{7,6},{8,9},{9,8},{10,11... | collective-permute-start | bytes 1376264 | tf_op jit(solution)/shard_map/ppermute | solution.py:30
  33.8 1.4 collective-permute-done.other_ref
  35.2 2.4 %shard_map.17 = bf16[4,8,272,128]{3,2,1,0:T(8,128)(2,1)S(1)} custom-call(s32[1]{0:T(128)} %bitcast.core_ref, bf16[112,2048]{1,0:T(8,128)(2,1)S(1)} %squeeze.3.own_ref.x_ref, bf16[112,2048]{1,0:T(8,128)(2,1)S(1)} %collective-permute-done.other_ref), custom_call_target="tpu_custom_call" | custom-call | flops 528482304 | bytes 4194304 | tf_op jit(solution)/shard_map/pallas_call | solution.py:66
  37.6 75.3 %all_to_all.29 = bf16[32,272,128]{2,1,0:T(8,128)(2,1)S(1)} all-to-all(bf16[32,272,128]{2,1,0:T(8,128)(2,1)S(1)} %bitcast.4), channel_id=1, replica_groups=mesh['x'=8,'zl'=2,'zh'=4,'y'=8,'c'=2] {'zh','y'}, dimensions={0} | all-to-all | bytes 4456448 | tf_op jit(solution)/shard_map/all_to_all | solution.py:172
  112.9 0.3 reduce_sum.12
  113.2 0.3 broadcast_in_dim.13
  113.5 62.1 %all_to_all.30 = bf16[32,272,128]{2,1,0:T(8,128)(2,1)S(1)} all-to-all(bf16[32,272,128]{2,1,0:T(8,128)(2,1)S(1)} %broadcast_in_dim.13), channel_id=1, replica_groups=mesh['x'=8,'zl'=2,'zh'=4,'y'=8,'c'=2] {'zh','y'}, dimensions={0} | all-to-all | bytes 4456448 | tf_op jit(solution)/shard_map/all_to_all | solution.py:175
  175.6 4.5 %collective-permute-start.1 = (bf16[4,8,272,128]{3,2,1,0:T(8,128)(2,1)S(1)}, bf16[4,8,272,128]{3,2,1,0:T(8,128)(2,1)S(1)}, u32[]{:S(2)}, u32[]{:S(2)}) collective-permute-start(bf16[4,8,272,128]{3,2,1,0:T(8,128)(2,1)S(1)} %bitcast.5), channel_id=1, source_target_pairs={{0,1},{1,0},{2,3},{3,2},{4,5},{5,4},{6,7},{7,6},{8,9},{9,8},{10,11... | collective-permute-start | bytes 6684680 | tf_op jit(solution)/shard_map/ppermute | solution.py:30
  180.1 4.0 %collective-permute-done.1.other_ref = bf16[4,8,272,128]{3,2,1,0:T(8,128)(2,1)S(1)} collective-permute-done((bf16[4,8,272,128]{3,2,1,0:T(8,128)(2,1)S(1)}, bf16[4,8,272,128]{3,2,1,0:T(8,128)(2,1)S(1)}, u32[]{:S(2)}, u32[]{:S(2)}) %collective-permute-start.1) | collective-permute-done | bytes 2228256 | tf_op jit(solution)/shard_map/ppermute | solution.py:30
  184.0 8.7 %shard_map.18 = bf16[4,112,512]{2,1,0:T(8,128)(2,1)S(1)} custom-call(s32[1]{0:T(128)} %bitcast.core_ref, bf16[112,2048]{1,0:T(8,128)(2,1)S(1)} %squeeze.3.own_ref.x_ref, bf16[4,8,272,128]{3,2,1,0:T(8,128)(2,1)S(1)} %bitcast.6, bf16[4,8,272,128]{3,2,1,0:T(8,128)(2,1)S(1)} %collective-permute-done.1.other_ref), custom_call_target="tpu_custom_call" | custom-call | flops 1879048192 | bytes 5242880 | tf_op jit(solution)/shard_map/pallas_call | solution.py:143
  192.8 10.1 %all_to_all.31 = bf16[4,112,512]{2,1,0:T(8,128)(2,1)S(1)} all-to-all(bf16[4,112,512]{2,1,0:T(8,128)(2,1)S(1)} %shard_map.18), channel_id=1, replica_groups={{0,1,2,3},{4,5,6,7},{8,9,10,11},{12,13,14,15},{16,17,18,19},{20,21,22,2..., dimensions={0} | all-to-all | bytes 917504 | tf_op jit(solution)/shard_map/all_to_all | solution.py:163
  202.9 0.8 copy.6
Async XLA Ops:
  23.3 12.0 %collective-permute-start = (bf16[112,2048]{1,0:T(8,128)(2,1)S(1)}, bf16[112,2048]{1,0:T(8,128)(2,1)S(1)}, u32[]{:S(2)}, u32[]{:S(2)}) collective-permute-start(bf16[112,2048]{1,0:T(8,128)(2,1)S(1)} %squeeze.3.own_ref.x_ref), channel_id=1, source_target_pairs={{0,1},{1,0},{2,3},{3,2},{4,5},{5,4},{6,7},{7,6},{8,9},{9,8},{10,11... | collective-permute-start | bytes 1376264 | tf_op jit(solution)/shard_map/ppermute | solution.py:30
  175.6 8.4 %collective-permute-start.1 = (bf16[4,8,272,128]{3,2,1,0:T(8,128)(2,1)S(1)}, bf16[4,8,272,128]{3,2,1,0:T(8,128)(2,1)S(1)}, u32[]{:S(2)}, u32[]{:S(2)}) collective-permute-start(bf16[4,8,272,128]{3,2,1,0:T(8,128)(2,1)S(1)} %bitcast.5), channel_id=1, source_target_pairs={{0,1},{1,0},{2,3},{3,2},{4,5},{5,4},{6,7},{7,6},{8,9},{9,8},{10,11... | collective-permute-start | bytes 6684680 | tf_op jit(solution)/shard_map/ppermute | solution.py:30

commit v5 on v4

v5 whole, which is shorter than its diff:
```python
import functools
import math

import jax
import jax.numpy as jnp
from jax import lax
from jax.experimental import pallas as pl
from jax.experimental.pallas import tpu as pltpu
from jax.sharding import Mesh
from jax.sharding import PartitionSpec as P

D = 7168
MOE_FF = 2048
N_Y = 8
N_Z = 4
SIDE = 128
SLAB = SIDE // N_Z
STRIP = 8 * SIDE
PAIR = 10 * SIDE
TURN = 9 * SIDE
EXTRA = SIDE // 2 // N_Z
PIECE = 8 * SLAB + EXTRA
WIDE = MOE_FF + PAIR
SCALE = 0.2 * math.sqrt(max(D, MOE_FF))
BF = jnp.bfloat16
F32 = jnp.float32


def swap_cores(value):
    return lax.ppermute(value, "c", [(0, 1), (1, 0)])


def send_y(value, shift):
    return lax.ppermute(value, ("yh", "yl"), [(y, (y + shift) % N_Y) for y in range(N_Y)])


def strips_kernel(first_ref, *refs):
    out_ref, wide = refs[-2:]
    at = 0
    for ref in refs[:-2]:
        rows = ref.shape[0]
        wide[at : at + rows, 0:MOE_FF] = ref[...]
        wide[at : at + rows, MOE_FF : MOE_FF + 8 * SIDE] = ref[:, 0 : 8 * SIDE]
        at += rows

    def times(left, right, width):
        return lax.dot_general(
            wide[:, pl.ds(pl.multiple_of(left, SIDE), SIDE)],
            wide[:, pl.ds(pl.multiple_of(right, SIDE), width)],
            (((0,), (0,)), ((), ())), preferred_element_type=F32,
        )

    def strip(y, carry):
        start = (4 * y + first_ref[0]) * SIDE
        value = times(start, start, STRIP).astype(BF)
        low = (4 * lax.rem(y, 2) + first_ref[0]) * SIDE
        extra = times(low, low + 8 * SIDE, SIDE)
        extra = jnp.where(y < 2, extra[: SIDE // 2], extra[SIDE // 2 :]).astype(BF)
        for z in range(N_Z):
            for m in range(8):
                out_ref[z, y, m * SLAB : (m + 1) * SLAB] = value[
                    z * SLAB : (z + 1) * SLAB, m * SIDE : (m + 1) * SIDE
                ]
            out_ref[z, y, 8 * SLAB : PIECE] = extra[z * EXTRA : (z + 1) * EXTRA]
        return carry

    lax.fori_loop(0, N_Y // 2, strip, 0)


def make_strips(first, pieces):
    vmem = pl.BlockSpec(memory_space=pltpu.VMEM)
    rows = sum(piece.shape[0] for piece in pieces)
    return pl.pallas_call(
        strips_kernel,
        out_shape=jax.ShapeDtypeStruct((N_Z, N_Y // 2, PIECE, SIDE), BF),
        in_specs=[pl.BlockSpec(memory_space=pltpu.SMEM)] + [vmem] * len(pieces),
        out_specs=vmem,
        scratch_shapes=[pltpu.VMEM((rows, MOE_FF + 8 * SIDE), BF)],
        compiler_params=pltpu.CompilerParams(vmem_limit_bytes=32 * 2**20),
        cost_estimate=pl.CostEstimate(
            flops=rows * SIDE * TURN * N_Y, bytes_accessed=4 * 2**20, transcendentals=0
        ),
    )(first, *pieces)


def apply_kernel(where_ref, x_ref, *refs):
    out_ref, wide, acc, direct, turned = refs[6:]
    core, parity = where_ref[0], where_ref[1]

    def place(ref, half, odd, first_z):
        top = pl.multiple_of(half * SIDE, SIDE)

        def block(m):
            return pl.ds(pl.multiple_of(top + m * SIDE, SIDE), SIDE)

        for h in range(N_Y // 2):
            pair = 2 * h + odd
            low = 2 * (h % 2) + odd
            for j in range(ref.shape[0]):
                z = first_z + j
                at = pl.ds(pl.multiple_of(top + z * SLAB, SLAB), SLAB)
                for m in range(8):
                    value = ref[j, h, m * SLAB : (m + 1) * SLAB]
                    direct[pair, at, block(m)] = value
                    if m:
                        turned[pair, at, block(m - 1)] = value
                first = top + z * EXTRA + h // 2 * (SIDE // 2)
                at = pl.ds(pl.multiple_of(first, EXTRA), EXTRA)
                value = ref[j, h, 8 * SLAB : PIECE]
                direct[low, at, block(8)] = value
                turned[low, at, block(7)] = value

    for side, half in ((0, core), (3, 1 - core)):
        place(refs[side], half, parity, 0)
        place(refs[side + 1], half, 1 - parity, 0)
        place(refs[side + 2], half, 1 - parity, N_Z // 2)
    zero = jnp.zeros((SIDE, SIDE), BF)
    for i in range(N_Y):
        last = 9 if i < 4 else 8
        direct[i, 0:SIDE, last * SIDE : (last + 1) * SIDE] = zero
        direct[i, SIDE : 2 * SIDE, 0:SIDE] = zero
        turned[i, 0:SIDE, (last - 1) * SIDE : last * SIDE] = zero
        turned[i, SIDE : 2 * SIDE, 0:SIDE] = zero

    def times_gram(value):
        wide[:, 0:MOE_FF] = value
        wide[:, MOE_FF:WIDE] = value[:, 0:PAIR]
        acc[...] = jnp.zeros_like(acc)

        def step(width, i, carry):
            start = pl.multiple_of(i * 2 * SIDE, 2 * SIDE)
            acc[:, pl.ds(start, width)] += lax.dot_general(
                wide[:, pl.ds(start, 2 * SIDE)], direct[i, :, 0:width],
                (((1,), (0,)), ((), ())), preferred_element_type=F32,
            )
            acc[:, pl.ds(start, 2 * SIDE)] += lax.dot_general(
                wide[:, pl.ds(pl.multiple_of(start + SIDE, SIDE), width - SIDE)],
                turned[i, :, 0 : width - SIDE],
                (((1,), (1,)), ((), ())), preferred_element_type=F32,
            )
            return carry

        lax.fori_loop(0, 4, functools.partial(step, PAIR), 0)
        lax.fori_loop(4, N_Y, functools.partial(step, TURN), 0)
        return jnp.concatenate(
            [acc[:, 0:PAIR] + acc[:, MOE_FF:WIDE], acc[:, PAIR:MOE_FF]], axis=1
        )

    x = x_ref[...]
    first = times_gram(x).astype(BF)
    second = times_gram(first)
    fresh = SCALE * (3.4445 * x.astype(F32) - 4.775 * first.astype(F32) + 2.0315 * second)
    fresh = fresh.astype(BF)
    for q in range(4):
        out_ref[q] = fresh[:, q * 512 : (q + 1) * 512]


def apply_gram(where, x, pieces):
    rows = x.shape[0]
    vmem = pl.BlockSpec(memory_space=pltpu.VMEM)
    return pl.pallas_call(
        apply_kernel,
        out_shape=jax.ShapeDtypeStruct((4, rows, 512), BF),
        in_specs=[pl.BlockSpec(memory_space=pltpu.SMEM)] + [vmem] * 7,
        out_specs=vmem,
        scratch_shapes=[
            pltpu.VMEM((rows, WIDE), BF),
            pltpu.VMEM((rows, WIDE), F32),
            pltpu.VMEM((N_Y, 2 * SIDE, PAIR), BF),
            pltpu.VMEM((N_Y, 2 * SIDE, TURN), BF),
        ],
        compiler_params=pltpu.CompilerParams(vmem_limit_bytes=40 * 2**20),
        cost_estimate=pl.CostEstimate(
            flops=4 * rows * MOE_FF * MOE_FF, bytes_accessed=5 * 2**20, transcendentals=0
        ),
    )(where, x, *pieces)


def shards(iterate):
    core = lax.axis_index("c").astype(jnp.int32)
    parity = lax.axis_index("yl").astype(jnp.int32)
    own = lax.all_to_all(iterate, ("x", "zl"), split_axis=0, concat_axis=1, tiled=True)[0]
    half = own.shape[0] // 2
    near = jnp.concatenate([send_y(own[:half], 1), send_y(own[half:], -1)], 0)
    strips = make_strips((2 * parity + core)[None], [own, swap_cores(own), near, swap_cores(near)])
    count = N_Z * N_Y // 2
    strips = strips.reshape(count, PIECE, SIDE)
    parts = lax.all_to_all(strips, ("zh", "yh"), 0, 0, tiled=True)
    piece = parts.astype(F32).sum(0).astype(BF)
    copies = jnp.broadcast_to(piece[None], (count, PIECE, SIDE))
    same = lax.all_to_all(copies, ("zh", "yh"), 0, 0, tiled=True)
    same = same.reshape(N_Z, N_Y // 2, PIECE, SIDE)
    mine = [same, send_y(same[: N_Z // 2], 1), send_y(same[N_Z // 2 :], -1)]
    other = [swap_cores(value) for value in mine]
    fresh = apply_gram(jnp.stack([core, parity]), own, mine + other)
    out = lax.all_to_all(fresh, ("yl", "c"), 0, 1, tiled=True)
    return out[:, None]


def solution(mesh):
    names = ("x", "zl", "zh", "yh", "yl", "c")
    split = Mesh(mesh.devices.reshape(8, 2, N_Z, N_Y // 2, 2, 2), names)
    return jax.shard_map(
        shards,
        mesh=split,
        in_specs=(P(None, names, None),),
        out_specs=P(names[:2], names[2:], None, None),
        check_vma=False,
    )
```

time: 204 us -> 187 us (0.917)
  the two profiles are of different devices: /device:TPU:1 before, /device:TPU:6 now
where the time goes in v5:
time: 187 us; the launch traced here: 186 us
  blocking collectives  133 us (71%)
  starting transfers between devices  24.9 us (13%)
  waiting for transfers between devices  13.9 us (7%)
  Pallas kernels  11.6 us (6%)
  local copies, waits for them, and re-layouts  2.67 us (1%)
    all_to_all x1, blocking collectives, shards(): parts = lax.all_to_all(strips, ('zh', 'yh'), 0, 0, tiled=True)  51.5 us
    all_to_all x1, blocking collectives, shards(): same = lax.all_to_all(copies, ('zh', 'yh'), 0, 0, tiled=True)  40.9 us
    all_to_all x1, blocking collectives, shards(): lax.all_to_all(iterate, ('x', 'zl'), split_axis=0, concat_axis=1, tiled=T...  26.5 us
    ppermute x4, starting transfers between devices, send_y(): lax.ppermute(value, ('yh', 'yl'), [(y, (y + shift) % N_Y) for y in range(...  14.8 us
    all_to_all x1, blocking collectives, shards(): out = lax.all_to_all(fresh, ('yl', 'c'), 0, 1, tiled=True)  13.8 us
    ppermute x4, waiting for transfers between devices, send_y(): lax.ppermute(value, ('yh', 'yl'), [(y, (y + shift) % N_Y) for y in range(...  10.7 us
    ppermute x5, starting transfers between devices, swap_cores(): return lax.ppermute(value, 'c', [(0, 1), (1, 0)])  10.1 us
    pallas_call x1, Pallas kernels, apply_gram(): pl.pallas_call(apply_kernel, out_shape=jax.ShapeDtypeStruct((4, rows, 512...  9.98 us
  transfers between devices with their start and end apart: 9, of which 5 were waited for; matrix products, arithmetic and copies ran while one was open for 0% of the time, Pallas kernels for 0%

profile of v5, /device:TPU:6, one launch (start us, length us, event | category | flops | bytes accessed | tf_op | source)
XLA Modules:
  0.0 186.3 jit_solution(10306071537703037086)
XLA Ops:
  0.0 1.3 copy.8
  1.3 26.5 %all_to_all.28 = bf16[16,7,2048]{2,1,0:T(8,128)(2,1)S(1)} all-to-all(bf16[16,7,2048]{2,1,0:T(8,128)(2,1)S(1)} %copy.8), channel_id=1, replica_groups=mesh['x'=8,'zl'=2,'zh'=4,'yh'=4,'yl'=2,'c'=2] {'x','zl'}, dimensions={0} | all-to-all | bytes 917504 | tf_op jit(solution)/shard_map/all_to_all | solution.py:182
  27.9 0.1 slice.25
  27.9 2.0 %collective-permute-start.1 = (bf16[56,2048]{1,0:T(8,128)(2,1)S(1)}, bf16[56,2048]{1,0:T(8,128)(2,1)S(1)}, u32[]{:S(2)}, u32[]{:S(2)}) collective-permute-start(bf16[56,2048]{1,0:T(8,128)(2,1)S(1)} %slice.25), channel_id=1, source_target_pairs={{0,2},{2,4},{4,6},{6,8},{8,10},{10,12},{12,14},{14,0},{1,3},{3,5},... | collective-permute-start | bytes 688136 | tf_op jit(solution)/shard_map/ppermute | solution.py:34
  29.9 0.1 slice.27
  30.0 5.1 %collective-permute-start.2 = (bf16[56,2048]{1,0:T(8,128)(2,1)S(1)}, bf16[56,2048]{1,0:T(8,128)(2,1)S(1)}, u32[]{:S(2)}, u32[]{:S(2)}) collective-permute-start(bf16[56,2048]{1,0:T(8,128)(2,1)S(1)} %slice.27), channel_id=1, source_target_pairs={{0,14},{2,0},{4,2},{6,4},{8,6},{10,8},{12,10},{14,12},{1,15},{3,1}... | collective-permute-start | bytes 688136 | tf_op jit(solution)/shard_map/ppermute | solution.py:34
  35.1 0.2 squeeze.3.refs_0_.x_ref
  35.3 1.9 %collective-permute-start = (bf16[112,2048]{1,0:T(8,128)(2,1)S(1)}, bf16[112,2048]{1,0:T(8,128)(2,1)S(1)}, u32[]{:S(2)}, u32[]{:S(2)}) collective-permute-start(bf16[112,2048]{1,0:T(8,128)(2,1)S(1)} %squeeze.3.refs_0_.x_ref), channel_id=1, source_target_pairs={{0,1},{1,0},{2,3},{3,2},{4,5},{5,4},{6,7},{7,6},{8,9},{9,8},{10,11... | collective-permute-start | bytes 1376264 | tf_op jit(solution)/shard_map/ppermute | solution.py:30
  37.2 1.1 collective-permute-done.1
  38.3 1.3 collective-permute-done.2
  39.6 1.9 %collective-permute-start.3 = (bf16[112,2048]{1,0:T(8,128)(2,1)S(1)}, bf16[112,2048]{1,0:T(8,128)(2,1)S(1)}, u32[]{:S(2)}, u32[]{:S(2)}) collective-permute-start(bf16[112,2048]{1,0:T(8,128)(2,1)S(1)} %constant_dynamic-update-slice_fusion.refs_2_), channel_id=1, source_target_pairs={{0,1},{1,0},{2,3},{3,2},{4,5},{5,4},{6,7},{7,6},{8,9},{9,8},{10,11... | collective-permute-start | bytes 1376264 | tf_op jit(solution)/shard_map/ppermute | solution.py:30
  41.5 0.0 collective-permute-done.refs_1_
  41.5 1.8 collective-permute-done.3.refs_3_
  43.3 1.7 shard_map.17
  44.9 51.5 %all_to_all.29 = bf16[16,272,128]{2,1,0:T(8,128)(2,1)S(1)} all-to-all(bf16[16,272,128]{2,1,0:T(8,128)(2,1)S(1)} %bitcast.10), channel_id=1, replica_groups=mesh['x'=8,'zl'=2,'zh'=4,'yh'=4,'yl'=2,'c'=2] {'zh','yh'}, dimensions={0} | all-to-all | bytes 2228224 | tf_op jit(solution)/shard_map/all_to_all | solution.py:188
  96.5 0.2 reduce_sum.12
  96.6 0.1 broadcast_in_dim.13
  96.8 40.9 %all_to_all.30 = bf16[16,272,128]{2,1,0:T(8,128)(2,1)S(1)} all-to-all(bf16[16,272,128]{2,1,0:T(8,128)(2,1)S(1)} %broadcast_in_dim.13), channel_id=1, replica_groups=mesh['x'=8,'zl'=2,'zh'=4,'yh'=4,'yl'=2,'c'=2] {'zh','yh'}, dimensions={0} | all-to-all | bytes 2228224 | tf_op jit(solution)/shard_map/all_to_all | solution.py:191
  137.7 0.1 fusion
  137.7 4.0 %collective-permute-start.4 = (bf16[2,4,272,128]{3,2,1,0:T(8,128)(2,1)S(1)}, bf16[2,4,272,128]{3,2,1,0:T(8,128)(2,1)S(1)}, u32[]{:S(2)}, u32[]{:S(2)}) collective-permute-start(bf16[2,4,272,128]{3,2,1,0:T(8,128)(2,1)S(1)} %bitcast.13), channel_id=1, source_target_pairs={{0,2},{2,4},{4,6},{6,8},{8,10},{10,12},{12,14},{14,0},{1,3},{3,5},... | collective-permute-start | bytes 1671176 | tf_op jit(solution)/shard_map/ppermute | solution.py:34
  141.7 3.8 %collective-permute-start.5 = (bf16[2,4,272,128]{3,2,1,0:T(8,128)(2,1)S(1)}, bf16[2,4,272,128]{3,2,1,0:T(8,128)(2,1)S(1)}, u32[]{:S(2)}, u32[]{:S(2)}) collective-permute-start(bf16[2,4,272,128]{3,2,1,0:T(8,128)(2,1)S(1)} %bitcast.12), channel_id=1, source_target_pairs={{0,14},{2,0},{4,2},{6,4},{8,6},{10,8},{12,10},{14,12},{1,15},{3,1}... | collective-permute-start | bytes 1671176 | tf_op jit(solution)/shard_map/ppermute | solution.py:34
  145.5 1.9 %collective-permute-start.6 = (bf16[4,4,272,128]{3,2,1,0:T(8,128)(2,1)S(1)}, bf16[4,4,272,128]{3,2,1,0:T(8,128)(2,1)S(1)}, u32[]{:S(2)}, u32[]{:S(2)}) collective-permute-start(bf16[4,4,272,128]{3,2,1,0:T(8,128)(2,1)S(1)} %bitcast.8), channel_id=1, source_target_pairs={{0,1},{1,0},{2,3},{3,2},{4,5},{5,4},{6,7},{7,6},{8,9},{9,8},{10,11... | collective-permute-start | bytes 3342344 | tf_op jit(solution)/shard_map/ppermute | solution.py:30
  147.5 8.4 %collective-permute-done.4.refs_1_ = bf16[2,4,272,128]{3,2,1,0:T(8,128)(2,1)S(1)} collective-permute-done((bf16[2,4,272,128]{3,2,1,0:T(8,128)(2,1)S(1)}, bf16[2,4,272,128]{3,2,1,0:T(8,128)(2,1)S(1)}, u32[]{:S(2)}, u32[]{:S(2)}) %collective-permute-start.4) | collective-permute-done | bytes 557088 | tf_op jit(solution)/shard_map/ppermute | solution.py:34
  155.8 1.9 %collective-permute-start.7 = (bf16[2,4,272,128]{3,2,1,0:T(8,128)(2,1)S(1)}, bf16[2,4,272,128]{3,2,1,0:T(8,128)(2,1)S(1)}, u32[]{:S(2)}, u32[]{:S(2)}) collective-permute-start(bf16[2,4,272,128]{3,2,1,0:T(8,128)(2,1)S(1)} %collective-permute-done.4.refs_1_), channel_id=1, source_target_pairs={{0,1},{1,0},{2,3},{3,2},{4,5},{5,4},{6,7},{7,6},{8,9},{9,8},{10,11... | collective-permute-start | bytes 1671176 | tf_op jit(solution)/shard_map/ppermute | solution.py:30
  157.8 0.0 collective-permute-done.5.refs_2_
  157.8 2.4 %collective-permute-start.8 = (bf16[2,4,272,128]{3,2,1,0:T(8,128)(2,1)S(1)}, bf16[2,4,272,128]{3,2,1,0:T(8,128)(2,1)S(1)}, u32[]{:S(2)}, u32[]{:S(2)}) collective-permute-start(bf16[2,4,272,128]{3,2,1,0:T(8,128)(2,1)S(1)} %collective-permute-done.5.refs_2_), channel_id=1, source_target_pairs={{0,1},{1,0},{2,3},{3,2},{4,5},{5,4},{6,7},{7,6},{8,9},{9,8},{10,11... | collective-permute-start | bytes 1671176 | tf_op jit(solution)/shard_map/ppermute | solution.py:30
  160.2 0.1 pad_add_fusion.where_ref
  160.3 0.0 collective-permute-done.7.refs_4_
  160.3 1.5 collective-permute-done.8.refs_5_
  161.7 0.0 collective-permute-done.6.refs_3_
  161.7 10.0 %shard_map.18 = bf16[4,112,512]{2,1,0:T(8,128)(2,1)S(1)} custom-call(s32[2]{0:T(128)S(1)} %pad_add_fusion.where_ref, bf16[112,2048]{1,0:T(8,128)(2,1)S(1)} %squeeze.3.refs_0_.x_ref, bf16[4,4,272,128]{3,2,1,0:T(8,128)(2,1)S(1)} %bitcast.9, bf16[2,4,272,128]{3,2,1,0:T(8,128)(2,1)S(1)} %collective-permute-done.4.refs_1_, ...), custom_call_target="tpu_custom_call" | custom-call | flops 1879048192 | bytes 5242880 | tf_op jit(solution)/shard_map/pallas_call | solution.py:161
  171.7 13.8 %all_to_all.31 = bf16[4,112,512]{2,1,0:T(8,128)(2,1)S(1)} all-to-all(bf16[4,112,512]{2,1,0:T(8,128)(2,1)S(1)} %shard_map.18), channel_id=1, replica_groups=mesh['x'=8,'zl'=2,'zh'=4,'yh'=4,'yl'=2,'c'=2] {'yl','c'}, dimensions={0} | all-to-all | bytes 917504 | tf_op jit(solution)/shard_map/all_to_all | solution.py:196
  185.6 0.8 copy.11
  (3 shorter events, 0.1 us)
Async XLA Ops:
  27.9 10.3 %collective-permute-start.1 = (bf16[56,2048]{1,0:T(8,128)(2,1)S(1)}, bf16[56,2048]{1,0:T(8,128)(2,1)S(1)}, u32[]{:S(2)}, u32[]{:S(2)}) collective-permute-start(bf16[56,2048]{1,0:T(8,128)(2,1)S(1)} %slice.25), channel_id=1, source_target_pairs={{0,2},{2,4},{4,6},{6,8},{8,10},{10,12},{12,14},{14,0},{1,3},{3,5},... | collective-permute-start | bytes 688136 | tf_op jit(solution)/shard_map/ppermute | solution.py:34
  30.0 9.5 %collective-permute-start.2 = (bf16[56,2048]{1,0:T(8,128)(2,1)S(1)}, bf16[56,2048]{1,0:T(8,128)(2,1)S(1)}, u32[]{:S(2)}, u32[]{:S(2)}) collective-permute-start(bf16[56,2048]{1,0:T(8,128)(2,1)S(1)} %slice.27), channel_id=1, source_target_pairs={{0,14},{2,0},{4,2},{6,4},{8,6},{10,8},{12,10},{14,12},{1,15},{3,1}... | collective-permute-start | bytes 688136 | tf_op jit(solution)/shard_map/ppermute | solution.py:34
  35.3 6.2 %collective-permute-start = (bf16[112,2048]{1,0:T(8,128)(2,1)S(1)}, bf16[112,2048]{1,0:T(8,128)(2,1)S(1)}, u32[]{:S(2)}, u32[]{:S(2)}) collective-permute-start(bf16[112,2048]{1,0:T(8,128)(2,1)S(1)} %squeeze.3.refs_0_.x_ref), channel_id=1, source_target_pairs={{0,1},{1,0},{2,3},{3,2},{4,5},{5,4},{6,7},{7,6},{8,9},{9,8},{10,11... | collective-permute-start | bytes 1376264 | tf_op jit(solution)/shard_map/ppermute | solution.py:30
  39.6 3.7 %collective-permute-start.3 = (bf16[112,2048]{1,0:T(8,128)(2,1)S(1)}, bf16[112,2048]{1,0:T(8,128)(2,1)S(1)}, u32[]{:S(2)}, u32[]{:S(2)}) collective-permute-start(bf16[112,2048]{1,0:T(8,128)(2,1)S(1)} %constant_dynamic-update-slice_fusion.refs_2_), channel_id=1, source_target_pairs={{0,1},{1,0},{2,3},{3,2},{4,5},{5,4},{6,7},{7,6},{8,9},{9,8},{10,11... | collective-permute-start | bytes 1376264 | tf_op jit(solution)/shard_map/ppermute | solution.py:30
  137.7 18.1 %collective-permute-start.4 = (bf16[2,4,272,128]{3,2,1,0:T(8,128)(2,1)S(1)}, bf16[2,4,272,128]{3,2,1,0:T(8,128)(2,1)S(1)}, u32[]{:S(2)}, u32[]{:S(2)}) collective-permute-start(bf16[2,4,272,128]{3,2,1,0:T(8,128)(2,1)S(1)} %bitcast.13), channel_id=1, source_target_pairs={{0,2},{2,4},{4,6},{6,8},{8,10},{10,12},{12,14},{14,0},{1,3},{3,5},... | collective-permute-start | bytes 1671176 | tf_op jit(solution)/shard_map/ppermute | solution.py:34
  141.7 16.0 %collective-permute-start.5 = (bf16[2,4,272,128]{3,2,1,0:T(8,128)(2,1)S(1)}, bf16[2,4,272,128]{3,2,1,0:T(8,128)(2,1)S(1)}, u32[]{:S(2)}, u32[]{:S(2)}) collective-permute-start(bf16[2,4,272,128]{3,2,1,0:T(8,128)(2,1)S(1)} %bitcast.12), channel_id=1, source_target_pairs={{0,14},{2,0},{4,2},{6,4},{8,6},{10,8},{12,10},{14,12},{1,15},{3,1}... | collective-permute-start | bytes 1671176 | tf_op jit(solution)/shard_map/ppermute | solution.py:34
  145.5 16.2 %collective-permute-start.6 = (bf16[4,4,272,128]{3,2,1,0:T(8,128)(2,1)S(1)}, bf16[4,4,272,128]{3,2,1,0:T(8,128)(2,1)S(1)}, u32[]{:S(2)}, u32[]{:S(2)}) collective-permute-start(bf16[4,4,272,128]{3,2,1,0:T(8,128)(2,1)S(1)} %bitcast.8), channel_id=1, source_target_pairs={{0,1},{1,0},{2,3},{3,2},{4,5},{5,4},{6,7},{7,6},{8,9},{9,8},{10,11... | collective-permute-start | bytes 3342344 | tf_op jit(solution)/shard_map/ppermute | solution.py:30
  155.8 4.4 %collective-permute-start.7 = (bf16[2,4,272,128]{3,2,1,0:T(8,128)(2,1)S(1)}, bf16[2,4,272,128]{3,2,1,0:T(8,128)(2,1)S(1)}, u32[]{:S(2)}, u32[]{:S(2)}) collective-permute-start(bf16[2,4,272,128]{3,2,1,0:T(8,128)(2,1)S(1)} %collective-permute-done.4.refs_1_), channel_id=1, source_target_pairs={{0,1},{1,0},{2,3},{3,2},{4,5},{5,4},{6,7},{7,6},{8,9},{9,8},{10,11... | collective-permute-start | bytes 1671176 | tf_op jit(solution)/shard_map/ppermute | solution.py:30
  157.8 4.0 %collective-permute-start.8 = (bf16[2,4,272,128]{3,2,1,0:T(8,128)(2,1)S(1)}, bf16[2,4,272,128]{3,2,1,0:T(8,128)(2,1)S(1)}, u32[]{:S(2)}, u32[]{:S(2)}) collective-permute-start(bf16[2,4,272,128]{3,2,1,0:T(8,128)(2,1)S(1)} %collective-permute-done.5.refs_2_), channel_id=1, source_target_pairs={{0,1},{1,0},{2,3},{3,2},{4,5},{5,4},{6,7},{7,6},{8,9},{9,8},{10,11... | collective-permute-start | bytes 1671176 | tf_op jit(solution)/shard_map/ppermute | solution.py:30
